TPU v7x, 32 devices: a whole 2x2x4 slice. The times are simulated.
32 devices in a mesh: seq: 16 (over z, x, core), tp: 2 (over y).
Axes of the slice: x: 2, y: 2, z: 4, core: 2. Of those that a mesh axis runs over, the one named last changes fastest.
Arguments:
- tokens: bfloat16 [8192, 4096], P('seq'), may hold values from -6 to 6
- w_in: bfloat16 [4096, 3, 4096], P('seq', None, 'tp'), may hold values from -0.09375 to 0.09375
- short_taps: float32 [3, 3, 4096], P(None, None, 'tp'), may hold values from -3 to 3
- decay_rate: float32 [256, 16], P('tp'), may hold values from 1.2207031e-05 to 0.04, as said below
- residue: float32 [256, 16], P('tp'), may hold values from -4 to 4
- skip_gain: float32 [4096], P('tp'), may hold values from -4 to 4
- w_out: bfloat16 [4096, 4096], P('tp'), may hold values from -0.125 to 0.125
Outputs:
- mixed: bfloat16 [8192, 4096], P('seq', 'tp')
Inputs may be any that keep to these rules, and one draw needn't show every extreme that they name: `decay_rate`: every decay rate is positive.
All inputs are finite; a program needn't handle non-finite values.
Results may differ from a plain program's by a relative error of at most 0.0075.
Values may be sent and summed in bfloat16 or wider, within the bound.
A program may use at most 192 MiB of HBM per device.

v0:
```python
import jax
import jax.numpy as jnp
from jax import lax
from jax.sharding import PartitionSpec as P

SUB = 128


def passed_along(block, axis, distance):
    devices = range(lax.axis_size(axis))
    route = [(i - distance, i) for i in devices if i - distance in devices]
    return lax.ppermute(block, axis, route)


def prefix(value, axis, combine, identity):
    peers, here = (lax.axis_size(axis), lax.axis_index(axis))
    everything = jax.tree.map(lambda part: lax.all_gather(part, axis), value)
    start = jax.tree.map(
        lambda part, zero: jnp.broadcast_to(jnp.asarray(zero, part.dtype), part.shape),
        value,
        identity,
    )

    def step(k, before):
        reached = k < here
        new = combine(before, jax.tree.map(lambda part: part[k], everything))
        return jax.tree.map(lambda a, b: jnp.where(reached, a, b), new, before)

    return lax.fori_loop(0, peers, step, start)


def shards(tokens, w_in, short_taps, decay_rate, residue, skip_gain, w_out):
    count = tokens.shape[0]
    chans = w_in.shape[2]
    groups = decay_rate.shape[0]
    order = decay_rate.shape[1]
    width = chans // groups
    taps = short_taps.shape[0]
    highest = lax.Precision.HIGHEST
    piece = lax.all_gather(w_in, "seq", axis=0, tiled=True)
    summed = jnp.dot(
        tokens, piece.reshape(piece.shape[0], 3 * chans), preferred_element_type=jnp.float32
    )
    proj = summed.astype(jnp.bfloat16).reshape(count, 3, chans)
    before = passed_along(proj[count - (taps - 1) :], "seq", 1)
    padded = jnp.concatenate([before, proj], axis=0).astype(jnp.float32)
    filtered = jnp.zeros((count, 3, chans), jnp.float32)
    for tap in range(taps):
        filtered = filtered + short_taps[tap] * padded[taps - 1 - tap : taps - 1 - tap + count]
    query = filtered[:, 0]
    gated = filtered[:, 1] * filtered[:, 2]
    weight_mode = residue * jnp.sqrt(2.0 * decay_rate / order)
    offsets = jnp.arange(SUB, dtype=jnp.float32)
    kernel = jnp.einsum(
        "gm,gmd->gd",
        weight_mode,
        jnp.exp(-decay_rate[:, :, None] * offsets[None, None, :]),
        precision=highest,
    )
    lag = jnp.arange(SUB)[:, None] - jnp.arange(SUB)[None, :]
    toeplitz = jnp.where(lag[None] >= 0, kernel[:, jnp.maximum(lag, 0)], 0.0)
    enter = weight_mode[:, None, :] * jnp.exp(
        -decay_rate[:, None, :] * (offsets[None, :, None] + 1.0)
    )
    leave = jnp.exp(-decay_rate[:, :, None] * (SUB - 1.0 - offsets[None, None, :]))
    fade = jnp.exp(-decay_rate * SUB)[:, :, None]
    blocks = gated.reshape(count // SUB, SUB, groups, width)

    def advance(state, block):
        local = jnp.einsum("gij,jgc->igc", toeplitz, block, precision=highest)
        local = local + jnp.einsum("gim,gmc->igc", enter, state, precision=highest)
        state = fade * state + jnp.einsum("gmj,jgc->gmc", leave, block, precision=highest)
        return (state, local)

    final_state, local_out = lax.scan(
        advance, jnp.zeros((groups, order, width), jnp.float32), blocks
    )
    local_out = local_out.reshape(count, groups, width)

    def combine(earlier, later):
        return (earlier[0] * later[0], later[1] + later[0][:, :, None] * earlier[1])

    hop = jnp.exp(-decay_rate * count)
    _, entering = prefix(
        (hop, final_state), "seq", combine, (jnp.ones_like(hop), jnp.zeros_like(final_state))
    )
    positions = jnp.arange(count, dtype=jnp.float32)
    reach = weight_mode[:, None, :] * jnp.exp(
        -decay_rate[:, None, :] * (positions[None, :, None] + 1.0)
    )
    carried = jnp.einsum("gtm,gmc->tgc", reach, entering, precision=highest)
    conv = (local_out + carried).reshape(count, chans)
    mix = (query * (conv + skip_gain * gated)).astype(jnp.bfloat16)
    partial_value = jnp.dot(mix, w_out, preferred_element_type=jnp.float32)
    return lax.psum_scatter(
        partial_value.astype(jnp.bfloat16), "tp", scatter_dimension=1, tiled=True
    )


def solution(mesh):
    in_specs = (
        P("seq", None),
        P("seq", None, "tp"),
        P(None, None, "tp"),
        P("tp", None),
        P("tp", None),
        P("tp"),
        P("tp", None),
    )
    out_specs = P("seq", "tp")
    return jax.shard_map(shards, mesh=mesh, in_specs=in_specs, out_specs=out_specs, check_vma=False)
```

profile of v0, /device:TPU:0, one launch (start us, length us, event | category | flops | bytes accessed | tf_op | source)
XLA Modules:
  0.0 692.5 jit_solution(16612572888679851134)
XLA Ops:
  12.4 54.7 %gather_fusion = f32[16384,128]{1,0:T(8,128)} fusion(f32[128,128]{0,1:T(8,128)S(1)} %copy.62, s32[16384]{0:T(1024)S(1)} %bitcast_clamp_fusion), kind=kCustom, calls=%fused_computation | custom fusion | bytes 16842752 | tf_op jit(solution)/shard_map/gather | solution.py:61
  67.2 9.4 %copy.50 = f32[128,128,128]{1,0,2:T(8,128)} copy(f32[128,128,128]{2,1,0:T(8,128)} %bitcast.89) | data formatting | bytes 16777216 | tf_op jit(solution)/shard_map/gather | solution.py:61
  76.6 8.3 %select_bitcast_fusion = f32[128,128,128]{2,1,0:T(8,128)} fusion(f32[128,128,128]{1,0,2:T(8,128)} %copy.50, pred[128,128]{1,0:T(8,128)(4,1)S(1)} %subtract_compare_fusion), kind=kLoop, calls=%fused_computation.30 | loop fusion | flops 2097152 | bytes 16793600 | tf_op jit(solution)/shard_map/jit(_where)/select_n | solution.py:61
  84.9 185.2 %all-gather.5.cloned.1.call-done = bf16[4096,3,2048]{0,2,1:T(8,128)(2,1)} async-done(((bf16[256,3,2048]{0,2,1:T(8,128)(2,1)}), bf16[4096,3,2048]{0,2,1:T(8,128)(2,1)}) %all-gather.5.cloned.1.call-update) | async-done | bytes 50331664 | tf_op jit(solution)/shard_map/all_gather | solution.py:40
  270.1 33.7 %convolution_convert_fusion = bf16[512,6144]{1,0:T(8,128)(2,1)} fusion(bf16[512,4096]{1,0:T(8,128)(2,1)} %param.11, bf16[4096,6144]{0,1:T(8,128)(2,1)} %bitcast.96), kind=kOutput, calls=%fused_computation.29 | convolution fusion | flops 25772949504 | bytes 60817408 | tf_op jit(solution)/shard_map/dot_general | solution.py:41
  307.2 8.7 %copy.47 = bf16[512,6144]{0,1:T(8,128)(2,1)} copy(bf16[512,6144]{1,0:T(8,128)(2,1)} %convolution_convert_fusion) | data formatting | bytes 12582912 | tf_op jit(solution)/shard_map/convert_element_type | solution.py:44
  316.7 11.7 %maximum_convert_fusion = f32[514,3,2048]{0,2,1:T(8,128)} fusion(bf16[512,3,2048]{0,2,1:T(8,128)(2,1)} %bitcast.90, bf16[2,3,2048]{0,2,1:T(8,128)(2,1)S(1)} %copy.48), kind=kLoop, calls=%fused_computation.31 | loop fusion | flops 12632064 | bytes 18948096 | tf_op jit(solution)/shard_map/convert_element_type | solution.py:46
  328.4 17.5 %fusion.19 = f32[512,3,2048]{0,2,1:T(8,128)S(1)} fusion(f32[514,3,2048]{0,2,1:T(8,128)} %maximum_convert_fusion, f32[3,2048]{1,0:T(4,128)S(1)} %get-tuple-element.340, f32[3,2048]{1,0:T(4,128)S(1)} %get-tuple-element.341, f32[3,2048]{1,0:T(4,128)S(1)} %get-tuple-element.339), kind=kLoop, calls=%fused_computation.25 | loop fusion | flops 15728640 | bytes 50405376 | tf_op jit(solution)/shard_map/add | solution.py:49
  353.4 5.2 mul.180
  358.6 198.3 %while.30 = (s32[]{:T(128)}, f32[128,16,16]{1,2,0:T(8,128)S(1)}, f32[4,128,128,16]{1,0,3,2:T(4,128)}, f32[128,16,1]{1,0,2:T(8,128)S(1)}, f32[4,128,128,16]{1,0,3...) while((s32[]{:T(128)}, f32[128,16,16]{1,2,0:T(8,128)S(1)}, ...), condition=%wide.region_1.2_spmd.clone.clone.clone, body=%wide.region_0.1_spmd.clone.clone.clone.sunk | while | flops 504496128 | bytes 18252936 | solution.py:75
  362.0 15.4 %fusion.57 = f32[128,16,128]{2,1,0:T(8,128)S(1)} fusion(f32[128,128,16]{0,2,1:T(8,128)S(1)} %bitcast.86, f32[128,128,128]{2,1,0:T(8,128)} %get-tuple-element.468), kind=kOutput, calls=%fused_computation.59.clone.1 | convolution fusion | flops 402653184 | bytes 10485760 | tf_op jit(solution)/shard_map/while/body/eval_jaxpr/gij,jgc->igc/dot_general | solution.py:70
  379.7 26.6 %dynamic_update_slice.8 = f32[4,128,128,16]{1,0,3,2:T(4,128)} dynamic-update-slice(f32[4,128,128,16]{1,0,3,2:T(4,128)} %get-tuple-element.453, f32[1,128,128,16]{1,0,3,2:T(1,128)} %bitcast.88, s32[]{:T(128)} %get-tuple-element.451, s32[]{:T(128)} %constant.52.clone.1..sunk.1, s32[]{:T(128)} %constant.52.clone.1..sunk.1, s32[]{:T(128)} %constant.52.clone.1..sunk.1) | dynamic-update-slice | bytes 2097156 | tf_op jit(solution)/shard_map/while/body/jit(dynamic_update_index_in_dim)/dynamic_update_slice | solution.py:75
  411.5 15.4 %fusion.57 = f32[128,16,128]{2,1,0:T(8,128)S(1)} fusion(f32[128,128,16]{0,2,1:T(8,128)S(1)} %bitcast.86, f32[128,128,128]{2,1,0:T(8,128)} %get-tuple-element.468), kind=kOutput, calls=%fused_computation.59.clone.1 | convolution fusion | flops 402653184 | bytes 10485760 | tf_op jit(solution)/shard_map/while/body/eval_jaxpr/gij,jgc->igc/dot_general | solution.py:70
  429.3 26.6 %dynamic_update_slice.8 = f32[4,128,128,16]{1,0,3,2:T(4,128)} dynamic-update-slice(f32[4,128,128,16]{1,0,3,2:T(4,128)} %get-tuple-element.453, f32[1,128,128,16]{1,0,3,2:T(1,128)} %bitcast.88, s32[]{:T(128)} %get-tuple-element.451, s32[]{:T(128)} %constant.52.clone.1..sunk.1, s32[]{:T(128)} %constant.52.clone.1..sunk.1, s32[]{:T(128)} %constant.52.clone.1..sunk.1) | dynamic-update-slice | bytes 2097156 | tf_op jit(solution)/shard_map/while/body/jit(dynamic_update_index_in_dim)/dynamic_update_slice | solution.py:75
  461.1 15.4 %fusion.57 = f32[128,16,128]{2,1,0:T(8,128)S(1)} fusion(f32[128,128,16]{0,2,1:T(8,128)S(1)} %bitcast.86, f32[128,128,128]{2,1,0:T(8,128)} %get-tuple-element.468), kind=kOutput, calls=%fused_computation.59.clone.1 | convolution fusion | flops 402653184 | bytes 10485760 | tf_op jit(solution)/shard_map/while/body/eval_jaxpr/gij,jgc->igc/dot_general | solution.py:70
  478.9 26.6 %dynamic_update_slice.8 = f32[4,128,128,16]{1,0,3,2:T(4,128)} dynamic-update-slice(f32[4,128,128,16]{1,0,3,2:T(4,128)} %get-tuple-element.453, f32[1,128,128,16]{1,0,3,2:T(1,128)} %bitcast.88, s32[]{:T(128)} %get-tuple-element.451, s32[]{:T(128)} %constant.52.clone.1..sunk.1, s32[]{:T(128)} %constant.52.clone.1..sunk.1, s32[]{:T(128)} %constant.52.clone.1..sunk.1) | dynamic-update-slice | bytes 2097156 | tf_op jit(solution)/shard_map/while/body/jit(dynamic_update_index_in_dim)/dynamic_update_slice | solution.py:75
  510.7 15.4 %fusion.57 = f32[128,16,128]{2,1,0:T(8,128)S(1)} fusion(f32[128,128,16]{0,2,1:T(8,128)S(1)} %bitcast.86, f32[128,128,128]{2,1,0:T(8,128)} %get-tuple-element.468), kind=kOutput, calls=%fused_computation.59.clone.1 | convolution fusion | flops 402653184 | bytes 10485760 | tf_op jit(solution)/shard_map/while/body/eval_jaxpr/gij,jgc->igc/dot_general | solution.py:70
  528.5 26.6 %dynamic_update_slice.8 = f32[4,128,128,16]{1,0,3,2:T(4,128)} dynamic-update-slice(f32[4,128,128,16]{1,0,3,2:T(4,128)} %get-tuple-element.453, f32[1,128,128,16]{1,0,3,2:T(1,128)} %bitcast.88, s32[]{:T(128)} %get-tuple-element.451, s32[]{:T(128)} %constant.52.clone.1..sunk.1, s32[]{:T(128)} %constant.52.clone.1..sunk.1, s32[]{:T(128)} %constant.52.clone.1..sunk.1) | dynamic-update-slice | bytes 2097156 | tf_op jit(solution)/shard_map/while/body/jit(dynamic_update_index_in_dim)/dynamic_update_slice | solution.py:75
  558.2 23.8 %all-gather.1 = f32[2048,16]{1,0:T(8,128)S(1)} all-gather(f32[128,16]{1,0:T(8,128)S(1)} %get-tuple-element.342), channel_id=3, replica_groups=mesh['seq'=16,'tp'=2] {'seq'}, dimensions={0}, use_global_device_ids=true | all-gather | bytes 139264 | tf_op jit(solution)/shard_map/all_gather | solution.py:17
  582.3 5.7 reshape.75
  588.0 12.8 %all-gather.7.cloned.1.call-done = f32[2048,16,16]{0,2,1:T(8,128)} async-done(((f32[128,16,16]{0,2,1:T(8,128)}), f32[2048,16,16]{0,2,1:T(8,128)}) %all-gather.7.cloned.1.call-update) | async-done | bytes 2097168 | tf_op jit(solution)/shard_map/all_gather | solution.py:17
  607.2 6.0 bitcast_add_fusion
  618.3 14.0 %convolution_convert_fusion.1 = bf16[512,4096]{1,0:T(8,128)(2,1)} fusion(bf16[512,2048]{0,1:T(8,128)(2,1)S(1)} %fusion.22, bf16[2048,4096]{1,0:T(8,128)(2,1)} %param.17), kind=kOutput, calls=%fused_computation.32 | convolution fusion | flops 8592031744 | bytes 23068672 | tf_op jit(solution)/shard_map/dot_general | solution.py:94
  632.3 53.6 %reduce-scatter.2.cloned.1.call-done = bf16[512,2048]{1,0:T(8,128)(2,1)} async-done(((bf16[512,4096]{1,0:T(8,128)(2,1)}), bf16[512,2048]{1,0:T(8,128)(2,1)}) %reduce-scatter.2.cloned.1.call-update) | async-done | bytes 2097168 | tf_op jit(solution)/shard_map/reduce_scatter | solution.py:95
  (103 shorter events, 64.2 us)
Async XLA Ops:
  6.5 4.9 copy-start.2
  6.5 5.0 copy-start.4
  6.5 263.6 %all-gather.5.cloned.1.call-start = ((), (), s32[]{:S(2)}) async-start(), calls=%async_computation.1 | async-start | bytes 53477376 | tf_op jit(solution)/shard_map/all_gather | solution.py:40
  11.3 589.5 %all-gather.7.cloned.1.call-start = ((), (), s32[]{:S(2)}) async-start(), calls=%async_computation.3 | async-start | bytes 2228224 | tf_op jit(solution)/shard_map/all_gather | solution.py:17
  67.2 9.4 %copy-start.1 = (f32[3,3,2048]{2,1,0:T(4,128)S(1)}, f32[3,3,2048]{2,1,0:T(4,128)}, u32[]{:S(2)}) copy-start(f32[3,3,2048]{2,1,0:T(4,128)} %param.13) | copy-start | bytes 221188
  304.8 11.0 %collective-permute-start = (bf16[2,3,2048]{2,1,0:T(4,128)(2,1)S(1)}, bf16[2,3,2048]{2,1,0:T(4,128)(2,1)S(1)}, u32[]{:S(2)}, u32[]{:S(2)}) collective-permute-start(bf16[2,3,2048]{2,1,0:T(4,128)(2,1)S(1)} %slice.35), channel_id=1, source_target_pairs={{0,2},{2,4},{4,6},{6,8},{8,10},{10,12},{12,14},{14,16},{16,18},{18... | collective-permute-start | bytes 73736 | tf_op jit(solution)/shard_map/ppermute | solution.py:12
  345.9 4.5 copy-start
  558.1 127.8 %reduce-scatter.2.cloned.1.call-start = ((), (), s32[]{:S(2)}) async-start(), calls=%async_computation.2 | async-start | bytes 6291456 | tf_op jit(solution)/shard_map/reduce_scatter | solution.py:95
  607.2 6.0 copy-start.3
Sparse Core Ops, SparseCore 0:
  11.5 258.6 all-gather.4
  558.2 42.5 all-gather.6
  632.4 53.4 reduce-scatter.1
where the time goes:
time: 696 us; the launch traced here: 692 us
  waiting for transfers between devices  252 us (36%)
  local copies, waits for them, and re-layouts  220 us (32%)
  matrix products  132 us (19%)
  other arithmetic  47.8 us (7%)
  blocking collectives  23.8 us (3%)
  between operations  13.3 us (2%)
    all_gather x1, waiting for transfers between devices, shards(): piece = lax.all_gather(w_in, 'seq', axis=0, tiled=True)  185 us
    dynamic_update_slice x4, local copies, waits for them, and re-layouts, shards(): lax.scan(advance, jnp.zeros((groups, order, width), jnp.float32), blocks)  106 us
    gather x2, local copies, waits for them, and re-layouts, shards(): toeplitz = jnp.where(lag[None] >= 0, kernel[:, jnp.maximum(lag, 0)], 0.0)  64.1 us
    dot_general x4, matrix products, advance(): local = jnp.einsum('gij,jgc->igc', toeplitz, block, precision=highest)  61.5 us
    reduce_scatter x1, waiting for transfers between devices, shards(): lax.psum_scatter(partial_value.astype(jnp.bfloat16), 'tp', scatter_dimens...  53.6 us
    dot_general x1, matrix products, shards(): jnp.dot(tokens, piece.reshape(piece.shape[0], 3 * chans), preferred_eleme...  33.7 us
    all_gather x1, blocking collectives, prefix(): everything = jax.tree.map(lambda part: lax.all_gather(part, axis), value)  23.8 us
    add x1, other arithmetic, shards(): filtered + short_taps[tap] * padded[taps - 1 - tap:taps - 1 - tap + count]  17.5 us
  transfers between devices with their start and end apart: 4, of which 3 were waited for; matrix products, arithmetic and copies ran while one was open for 13% of the time, Pallas kernels for 0%

commit v1 on v0

v1 whole, which is shorter than its diff:
```python
import functools

import jax
import jax.numpy as jnp
from jax import lax
from jax.experimental import pallas as pl
from jax.experimental.pallas import tpu as pltpu
from jax.sharding import PartitionSpec as P

SUB = 128
LANES = 256
CHUNK = 512
HALO = 16
MESH = pl.DeviceIdType.MESH
HIGHEST = lax.Precision.HIGHEST


def shifted_by(block, axis, distance):
    devices = range(lax.axis_size(axis))
    route = [(i - distance, i) for i in devices if i - distance in devices]
    return lax.ppermute(block, axis, route)


def rotated(block, axis, distance):
    size = lax.axis_size(axis)
    return lax.ppermute(block, axis, [(i, (i + distance) % size) for i in range(size)])


def fanned(state, width, order):
    lanes = state.shape[1]
    tile = lanes // width
    full = jnp.concatenate([state] * tile, axis=0)
    row = lax.broadcasted_iota(jnp.int32, full.shape, 0) // order
    lane = lax.broadcasted_iota(jnp.int32, full.shape, 1) // width
    return jnp.where(row == lane, full, 0.0)


def conv_kernel(
    width, q_ref, k_ref, v_ref, taps_ref, toep_ref, leave_ref, reach_ref, fade_ref, skip_ref,
    query_ref, base_ref, state_ref
):
    taps = taps_ref.shape[0]
    count, lanes = query_ref.shape
    order = state_ref.shape[0]
    tile = lanes // width

    def filtered(ref, which):
        value = ref[...].astype(jnp.float32)
        total = None
        for tap in range(taps):
            term = taps_ref[tap, which][None, :] * value[HALO - tap : HALO - tap + count]
            total = term if total is None else total + term
        return total

    query_ref[...] = filtered(q_ref, 0)
    gated = filtered(k_ref, 1) * filtered(v_ref, 2)
    lane = lax.broadcasted_iota(jnp.int32, (SUB, lanes), 1) // width
    row = lax.broadcasted_iota(jnp.int32, (tile * order, lanes), 0) // order
    diagonal = row == lax.broadcasted_iota(jnp.int32, (tile * order, lanes), 1) // width
    toep = toep_ref[...].reshape(tile * SUB, SUB)
    state = jnp.zeros((tile * order, lanes), jnp.float32)
    for block in range(count // SUB):
        piece = gated[block * SUB : (block + 1) * SUB]
        wide = jnp.dot(toep, piece.astype(jnp.bfloat16), preferred_element_type=jnp.float32)
        local = skip_ref[...] * piece
        picked = wide[:SUB]
        for g in range(1, tile):
            picked = jnp.where(lane == g, wide[g * SUB : (g + 1) * SUB], picked)
        local = local + picked
        if block:
            local = local + jnp.dot(
                reach_ref[:SUB], state, precision=HIGHEST, preferred_element_type=jnp.float32
            )
        base_ref[block * SUB : (block + 1) * SUB] = local
        fresh = jnp.dot(
            leave_ref[...], piece, precision=HIGHEST, preferred_element_type=jnp.float32
        )
        state = fade_ref[...] * state + jnp.where(diagonal, fresh, 0.0)
    compact = state[:order]
    for g in range(1, tile):
        compact = compact + state[g * order : (g + 1) * order]
    state_ref[...] = compact


def convolved(proj, taps, toep, leave, reach, fade, skip, width, order, count):
    chans = skip.shape[1]
    lanes = min(LANES, chans)
    steps = chans // lanes
    tile = lanes // width
    rows = proj.shape[0]
    return pl.pallas_call(
        functools.partial(conv_kernel, width),
        grid=(steps,),
        in_specs=[
            pl.BlockSpec((rows, lanes), lambda i: (0, i)),
            pl.BlockSpec((rows, lanes), lambda i: (0, steps + i)),
            pl.BlockSpec((rows, lanes), lambda i: (0, 2 * steps + i)),
            pl.BlockSpec((taps.shape[0], 3, lanes), lambda i: (0, 0, i)),
            pl.BlockSpec((tile, SUB, SUB), lambda i: (i, 0, 0)),
            pl.BlockSpec((tile * order, SUB), lambda i: (i, 0)),
            pl.BlockSpec((count, tile * order), lambda i: (0, i)),
            pl.BlockSpec((tile * order, 1), lambda i: (i, 0)),
            pl.BlockSpec((1, lanes), lambda i: (0, i)),
        ],
        out_specs=[
            pl.BlockSpec((count, lanes), lambda i: (0, i)),
            pl.BlockSpec((count, lanes), lambda i: (0, i)),
            pl.BlockSpec((order, lanes), lambda i: (0, i)),
        ],
        out_shape=[
            jax.ShapeDtypeStruct((count, chans), jnp.float32),
            jax.ShapeDtypeStruct((count, chans), jnp.float32),
            jax.ShapeDtypeStruct((order, chans), jnp.float32),
        ],
        cost_estimate=pl.CostEstimate(
            flops=2 * count * chans * SUB * tile, bytes_accessed=count * chans * 20, transcendentals=0
        ),
        name="conv",
    )(proj, proj, proj, taps, toep, leave, reach, fade, skip)


def share_kernel(own_ref, all_ref, send_sems, recv_sems):
    size = all_ref.shape[0]
    here = lax.axis_index("seq")
    barrier = pltpu.get_barrier_semaphore()
    for d in range(1, size):
        pl.semaphore_signal(
            barrier, inc=1, device_id={"seq": lax.rem(here + d, size)}, device_id_type=MESH
        )
    pl.semaphore_wait(barrier, size - 1)
    copies = []
    for d in range(1, size):
        copy = pltpu.make_async_remote_copy(
            src_ref=own_ref,
            dst_ref=all_ref.at[here],
            send_sem=send_sems.at[d - 1],
            recv_sem=recv_sems.at[d - 1],
            device_id={"seq": lax.rem(here + d, size)},
            device_id_type=MESH,
        )
        copy.start()
        copies.append(copy)
    all_ref[here] = own_ref[...]
    for copy in copies:
        copy.wait()


def shared(state):
    size = lax.axis_size("seq")
    return pl.pallas_call(
        share_kernel,
        out_shape=jax.ShapeDtypeStruct((size,) + state.shape, state.dtype),
        in_specs=[pl.BlockSpec(memory_space=pltpu.VMEM)],
        out_specs=pl.BlockSpec(memory_space=pltpu.VMEM),
        scratch_shapes=[
            pltpu.SemaphoreType.DMA((size - 1,)),
            pltpu.SemaphoreType.DMA((size - 1,)),
        ],
        compiler_params=pltpu.CompilerParams(collective_id=0, has_side_effects=True),
        cost_estimate=pl.CostEstimate(
            flops=0, bytes_accessed=40 * size * state.size, transcendentals=0
        ),
        name="share",
    )(state)


def mix_kernel(width, query_ref, base_ref, all_ref, weight_ref, reach_ref, mix_ref):
    order = all_ref.shape[1]
    entering = jnp.sum(all_ref[...] * weight_ref[...], axis=0)
    carried = jnp.dot(
        reach_ref[...],
        fanned(entering, width, order),
        precision=HIGHEST,
        preferred_element_type=jnp.float32,
    )
    mix_ref[...] = (query_ref[...] * (base_ref[...] + carried)).astype(mix_ref.dtype)


def mixed_of(query, base, everything, weight, reach, width):
    count, chans = query.shape
    size, order, _ = everything.shape
    lanes = min(LANES, chans)
    cols = lanes // width * order
    return pl.pallas_call(
        functools.partial(mix_kernel, width),
        grid=(chans // lanes,),
        in_specs=[
            pl.BlockSpec((count, lanes), lambda i: (0, i)),
            pl.BlockSpec((count, lanes), lambda i: (0, i)),
            pl.BlockSpec((size, order, lanes), lambda i: (0, 0, i)),
            pl.BlockSpec((size, order, lanes), lambda i: (0, 0, i)),
            pl.BlockSpec((count, cols), lambda i: (0, i)),
        ],
        out_specs=pl.BlockSpec((count, lanes), lambda i: (0, i)),
        out_shape=jax.ShapeDtypeStruct((count, chans), jnp.bfloat16),
        cost_estimate=pl.CostEstimate(
            flops=12 * count * chans * cols, bytes_accessed=count * chans * 10, transcendentals=0
        ),
        name="mix",
    )(query, base, everything, weight, reach)


def shards(tokens, w_in, short_taps, decay_rate, residue, skip_gain, w_out):
    count = tokens.shape[0]
    chans = w_in.shape[2]
    groups, order = decay_rate.shape
    width = chans // groups
    taps = short_taps.shape[0]
    size, here = lax.axis_size("seq"), lax.axis_index("seq")
    n_tp, part = lax.axis_size("tp"), lax.axis_index("tp")
    chunk = min(CHUNK, chans)
    chunks = chans // chunk

    pieces = []
    for c in range(chunks):
        cols = w_in[:, :, c * chunk : (c + 1) * chunk].reshape(w_in.shape[0], 3 * chunk)
        pieces.append(lax.all_gather(cols, "seq", axis=0, tiled=True))

    before = shifted_by(tokens[count - (taps - 1) :], "seq", 1)
    extended = jnp.concatenate(
        [jnp.zeros((HALO - (taps - 1), tokens.shape[1]), tokens.dtype), before, tokens], axis=0
    )

    out_cols = w_out.shape[1] // n_tp

    def columns_for(target):
        return lax.dynamic_slice_in_dim(w_out, target * out_cols, out_cols, axis=1)

    outs = [columns_for(part)]
    for d in range(1, n_tp):
        outs.append(rotated(columns_for((part + d) % n_tp), "tp", d))

    weight_mode = residue * jnp.sqrt(2.0 * decay_rate / order)
    offsets = jnp.arange(SUB, dtype=jnp.float32)
    kernel = jnp.einsum(
        "gm,gmd->gd",
        weight_mode,
        jnp.exp(-decay_rate[:, :, None] * offsets[None, None, :]),
        precision=HIGHEST,
    )
    lag = jnp.arange(SUB)[:, None] - jnp.arange(SUB)[None, :]
    toep = jnp.where(lag[None] >= 0, kernel[:, jnp.maximum(lag, 0)], 0.0).astype(jnp.bfloat16)
    rate = decay_rate.reshape(groups * order)
    leave = jnp.exp(-rate[:, None] * (SUB - 1.0 - offsets[None, :]))
    fade = jnp.exp(-rate * SUB)[:, None]
    positions = jnp.arange(count, dtype=jnp.float32)
    reach = weight_mode.reshape(groups * order)[None] * jnp.exp(
        -rate[None] * (positions[:, None] + 1.0)
    )
    by_mode = jnp.repeat(decay_rate.T, width, axis=1)
    ahead = (here - 1 - jnp.arange(size))[:, None, None]
    weight = jnp.where(
        ahead >= 0, jnp.exp(-by_mode[None] * (count * jnp.maximum(ahead, 0).astype(jnp.float32))), 0.0
    )
    skip = skip_gain[None]

    total = jnp.zeros((count, out_cols), jnp.float32)
    for c in range(chunks):
        lane = slice(c * chunk, (c + 1) * chunk)
        mode = slice(c * chunk // width * order, (c + 1) * chunk // width * order)
        group = slice(c * chunk // width, (c + 1) * chunk // width)
        proj = jnp.dot(extended, pieces[c], preferred_element_type=jnp.float32).astype(jnp.bfloat16)
        query, base, final = convolved(
            proj, short_taps[:, :, lane], toep[group], leave[mode], reach[:, mode], fade[mode],
            skip[:, lane], width, order, count,
        )
        everything = shared(final)
        mix = mixed_of(query, base, everything, weight[:, :, lane], reach[:, mode], width)
        for d in range(n_tp):
            block = mix if d == 0 else rotated(mix, "tp", d)
            total = total + jnp.dot(block, outs[d][lane], preferred_element_type=jnp.float32)
    return total.astype(jnp.bfloat16)


def solution(mesh):
    in_specs = (
        P("seq", None),
        P("seq", None, "tp"),
        P(None, None, "tp"),
        P("tp", None),
        P("tp", None),
        P("tp"),
        P("tp", None),
    )
    out_specs = P("seq", "tp")
    return jax.shard_map(shards, mesh=mesh, in_specs=in_specs, out_specs=out_specs, check_vma=False)
```

time: 696 us -> 583 us (0.84)
  Pallas kernels: 0 us -> 127 us
  local copies, waits for them, and re-layouts: 220 us -> 94.2 us
  matrix products: 132 us -> 86.9 us
  other arithmetic: 47.8 us -> 3.78 us
  blocking collectives: 23.8 us -> 0 us
  waiting for transfers between devices: 252 us -> 243 us
    pallas_call x0 -> x12, Pallas kernels: none -> 127 us  [the longest x4 75.1 us: shared(): pl.pallas_call(share_kernel, out_shape=jax.ShapeDtypeStruct((size,) + sta...]
    dynamic_update_slice x4 -> x0, local copies, waits for them, and re-layouts: 106 us -> none  [shards(): lax.scan(advance, jnp.zeros((groups, order, width), jnp.float32), blocks)]
    reduce_scatter x1 -> x0, waiting for transfers between devices: 53.6 us -> none  [shards(): lax.psum_scatter(partial_value.astype(jnp.bfloat16), 'tp', scatter_dimens...]
    dot_general x15 -> x12, matrix products: 132 us -> 86.9 us  [the longest x4 48.3 us: shards(): jnp.dot(extended, pieces[c], preferred_element_type=jnp.float32)]
    all_gather x2 -> x4, waiting for transfers between devices: 198 us -> 228 us  [shards(): pieces.append(lax.all_gather(cols, 'seq', axis=0, tiled=True))]
    all_gather x1 -> x0, blocking collectives: 23.8 us -> none  [prefix(): everything = jax.tree.map(lambda part: lax.all_gather(part, axis), value)]
    add x3 -> x1, other arithmetic: 17.5 us -> 0.01 us  [shards(): positions[:, None] + 1.0]
    convert_element_type x2 -> x1, other arithmetic: 16.8 us -> 1.75 us  [shards(): jnp.where(lag[None] >= 0, kernel[:, jnp.maximum(lag, 0)], 0.0)]
  transfers between devices with their start and end apart: 4 -> 10, of which waited for: 3 -> 6; matrix products, arithmetic and copies ran while one was open for 13% -> 30% of each run, Pallas kernels for 0% -> 22%
where the time goes in v1:
time: 583 us; the launch traced here: 578 us
  waiting for transfers between devices  243 us (42%)
  Pallas kernels  127 us (22%)
  local copies, waits for them, and re-layouts  94.2 us (16%)
  matrix products  86.9 us (15%)
  between operations  13.7 us (2%)
  starting transfers between devices  9.14 us (2%)
    all_gather x4, waiting for transfers between devices, shards(): pieces.append(lax.all_gather(cols, 'seq', axis=0, tiled=True))  228 us
    pallas_call x4, Pallas kernels, shared(): pl.pallas_call(share_kernel, out_shape=jax.ShapeDtypeStruct((size,) + sta...  75.1 us
    gather x2, local copies, waits for them, and re-layouts, shards(): kernel[:, jnp.maximum(lag, 0)]  64.7 us
    dot_general x4, matrix products, shards(): jnp.dot(extended, pieces[c], preferred_element_type=jnp.float32)  48.3 us
    dot_general x8, matrix products, shards(): jnp.dot(block, outs[d][lane], preferred_element_type=jnp.float32)  38.5 us
    pallas_call x4, Pallas kernels, convolved(): pl.pallas_call(functools.partial(conv_kernel, width), grid=(steps,), in_s...  37.2 us
    ppermute x5, waiting for transfers between devices, rotated(): lax.ppermute(block, axis, [(i, (i + distance) % size) for i in range(size)])  15 us
    pallas_call x4, Pallas kernels, mixed_of(): pl.pallas_call(functools.partial(mix_kernel, width), grid=(chans // lanes...  14.4 us
  transfers between devices with their start and end apart: 10, of which 6 were waited for; matrix products, arithmetic and copies ran while one was open for 30% of the time, Pallas kernels for 22%

profile of v1, /device:TPU:0, one launch (start us, length us, event | category | flops | bytes accessed | tf_op | source)
XLA Modules:
  0.0 577.6 jit_solution(9392750348852262582)
XLA Ops:
  17.0 8.5 %constant_dynamic-slice_fusion = bf16[2048,2048]{1,0:T(8,128)(2,1)} fusion(bf16[2048,4096]{1,0:T(8,128)(2,1)} %param.13, s32[]{:T(128)S(6)} %select_n.26), kind=kLoop, calls=%fused_computation.38 | loop fusion | bytes 16777220 | tf_op jit(solution)/shard_map/dynamic_slice | solution.py:227
  30.1 57.9 %gather_fusion = bf16[16384,128]{1,0:T(8,128)(2,1)} fusion(bf16[128,128]{0,1:T(8,128)(2,1)S(1)} %copy.25, s32[16384]{0:T(1024)S(1)} %bitcast_clamp_fusion), kind=kCustom, calls=%fused_computation | custom fusion | bytes 8454144 | tf_op jit(solution)/shard_map/gather | solution.py:242
  88.0 6.8 %copy.26 = bf16[128,128,128]{1,0,2:T(8,128)(2,1)} copy(bf16[128,128,128]{2,1,0:T(8,128)(2,1)} %bitcast.28) | data formatting | bytes 8388608 | tf_op jit(solution)/shard_map/gather | solution.py:242
  109.8 6.6 %all-gather.7.cloned.1.call-done = bf16[4096,1536]{0,1:T(8,128)(2,1)} async-done(((bf16[256,1536]{0,1:T(8,128)(2,1)}), bf16[4096,1536]{0,1:T(8,128)(2,1)}) %all-gather.7.cloned.1.call-update) | async-done | bytes 12582928 | tf_op jit(solution)/shard_map/all_gather | solution.py:217
  116.3 12.0 %convolution_convert_fusion.2.q_ref.k_ref.v_ref = bf16[528,1536]{1,0:T(8,128)(2,1)} fusion(bf16[4096,1536]{0,1:T(8,128)(2,1)} %all-gather.7.cloned.1.call-done, bf16[512,4096]{1,0:T(8,128)(2,1)} %param.7, bf16[2,4096]{1,0:T(2,128)(2,1)S(1)} %collective-permute-done, bf16[528]{0:T(1024)(128)(2,1)S(1)} %pad.clone), kind=kOutput, calls=%fused_computation.8 | convolution fusion | flops 6657564672 | bytes 18416672 | tf_op jit(solution)/shard_map/dot_general | solution.py:262
  128.4 9.3 %conv.5 = (f32[512,512]{1,0:T(8,128)}, f32[512,512]{1,0:T(8,128)}, f32[16,512]{1,0:T(8,128)}) custom-call(bf16[528,1536]{1,0:T(8,128)(2,1)} %convolution_convert_fusion.2.q_ref.k_ref.v_ref, bf16[528,1536]{1,0:T(8,128)(2,1)} %convolution_convert_fusion.2.q_ref.k_ref.v_ref, bf16[528,1536]{1,0:T(8,128)(2,1)} %convolution_convert_fusion.2.q_ref.k_ref.v_ref, ...), custom_call_target="tpu_custom_call" | custom-call | flops 1073741824 | bytes 5242880 | tf_op jit(solution)/shard_map/conv/pallas_call | solution.py:91
  137.6 20.7 %share.5.all_ref = f32[16,16,512]{2,1,0:T(8,128)} custom-call(f32[16,512]{1,0:T(8,128)} %get-tuple-element.22.own_ref), custom_call_target="tpu_custom_call" | custom-call | bytes 5242880 | tf_op jit(solution)/shard_map/share/pallas_call | solution.py:150
  158.3 73.9 %all-gather.9.cloned.1.call-done = bf16[4096,1536]{0,1:T(8,128)(2,1)} async-done(((bf16[256,1536]{0,1:T(8,128)(2,1)}), bf16[4096,1536]{0,1:T(8,128)(2,1)}) %all-gather.9.cloned.1.call-update) | async-done | bytes 12582928 | tf_op jit(solution)/shard_map/all_gather | solution.py:217
  232.3 12.2 %convolution_convert_fusion.1.q_ref.k_ref.v_ref = bf16[528,1536]{1,0:T(8,128)(2,1)} fusion(bf16[4096,1536]{0,1:T(8,128)(2,1)} %all-gather.9.cloned.1.call-done, bf16[512,4096]{1,0:T(8,128)(2,1)} %param.7, bf16[2,4096]{1,0:T(2,128)(2,1)S(1)} %collective-permute-done, bf16[528]{0:T(1024)(128)(2,1)S(1)} %pad.clone), kind=kOutput, calls=%fused_computation.7 | convolution fusion | flops 6657564672 | bytes 18416672 | tf_op jit(solution)/shard_map/dot_general | solution.py:262
  244.5 9.3 %conv.6 = (f32[512,512]{1,0:T(8,128)}, f32[512,512]{1,0:T(8,128)}, f32[16,512]{1,0:T(8,128)}) custom-call(bf16[528,1536]{1,0:T(8,128)(2,1)} %convolution_convert_fusion.1.q_ref.k_ref.v_ref, bf16[528,1536]{1,0:T(8,128)(2,1)} %convolution_convert_fusion.1.q_ref.k_ref.v_ref, bf16[528,1536]{1,0:T(8,128)(2,1)} %convolution_convert_fusion.1.q_ref.k_ref.v_ref, ...), custom_call_target="tpu_custom_call" | custom-call | flops 1073741824 | bytes 5242880 | tf_op jit(solution)/shard_map/conv/pallas_call | solution.py:91
  253.8 20.6 %share.6.all_ref = f32[16,16,512]{2,1,0:T(8,128)} custom-call(f32[16,512]{1,0:T(8,128)} %get-tuple-element.25.own_ref), custom_call_target="tpu_custom_call" | custom-call | bytes 5242880 | tf_op jit(solution)/shard_map/share/pallas_call | solution.py:150
  274.3 73.9 %all-gather.11.cloned.1.call-done = bf16[4096,1536]{0,1:T(8,128)(2,1)} async-done(((bf16[256,1536]{0,1:T(8,128)(2,1)}), bf16[4096,1536]{0,1:T(8,128)(2,1)}) %all-gather.11.cloned.1.call-update) | async-done | bytes 12582928 | tf_op jit(solution)/shard_map/all_gather | solution.py:217
  348.2 12.0 %convolution_convert_fusion.q_ref.k_ref.v_ref = bf16[528,1536]{1,0:T(8,128)(2,1)} fusion(bf16[4096,1536]{0,1:T(8,128)(2,1)} %all-gather.11.cloned.1.call-done, bf16[512,4096]{1,0:T(8,128)(2,1)} %param.7, bf16[2,4096]{1,0:T(2,128)(2,1)S(1)} %collective-permute-done, bf16[528]{0:T(1024)(128)(2,1)S(1)} %pad.clone), kind=kOutput, calls=%fused_computation.6 | convolution fusion | flops 6657564672 | bytes 18416672 | tf_op jit(solution)/shard_map/dot_general | solution.py:262
  360.2 9.4 %conv.7 = (f32[512,512]{1,0:T(8,128)}, f32[512,512]{1,0:T(8,128)}, f32[16,512]{1,0:T(8,128)}) custom-call(bf16[528,1536]{1,0:T(8,128)(2,1)} %convolution_convert_fusion.q_ref.k_ref.v_ref, bf16[528,1536]{1,0:T(8,128)(2,1)} %convolution_convert_fusion.q_ref.k_ref.v_ref, bf16[528,1536]{1,0:T(8,128)(2,1)} %convolution_convert_fusion.q_ref.k_ref.v_ref, ...), custom_call_target="tpu_custom_call" | custom-call | flops 1073741824 | bytes 5242880 | tf_op jit(solution)/shard_map/conv/pallas_call | solution.py:91
  369.7 20.5 %share.7.all_ref = f32[16,16,512]{2,1,0:T(8,128)} custom-call(f32[16,512]{1,0:T(8,128)} %get-tuple-element.28.own_ref), custom_call_target="tpu_custom_call" | custom-call | bytes 5242880 | tf_op jit(solution)/shard_map/share/pallas_call | solution.py:150
  390.2 73.8 %all-gather.5.cloned.1.call-done = bf16[4096,1536]{0,1:T(8,128)(2,1)} async-done(((bf16[256,1536]{0,1:T(8,128)(2,1)}), bf16[4096,1536]{0,1:T(8,128)(2,1)}) %all-gather.5.cloned.1.call-update) | async-done | bytes 12582928 | tf_op jit(solution)/shard_map/all_gather | solution.py:217
  463.9 12.0 %convolution_convert_fusion.3.q_ref.k_ref.v_ref = bf16[528,1536]{1,0:T(8,128)(2,1)} fusion(bf16[4096,1536]{0,1:T(8,128)(2,1)} %all-gather.5.cloned.1.call-done, bf16[512,4096]{1,0:T(8,128)(2,1)} %param.7, bf16[2,4096]{1,0:T(2,128)(2,1)S(1)} %collective-permute-done, bf16[528]{0:T(1024)(128)(2,1)S(1)} %pad.clone), kind=kOutput, calls=%fused_computation.9 | convolution fusion | flops 6657564672 | bytes 18416672 | tf_op jit(solution)/shard_map/dot_general | solution.py:262
  476.0 9.2 %conv.4 = (f32[512,512]{1,0:T(8,128)}, f32[512,512]{1,0:T(8,128)}, f32[16,512]{1,0:T(8,128)}) custom-call(bf16[528,1536]{1,0:T(8,128)(2,1)} %convolution_convert_fusion.3.q_ref.k_ref.v_ref, bf16[528,1536]{1,0:T(8,128)(2,1)} %convolution_convert_fusion.3.q_ref.k_ref.v_ref, bf16[528,1536]{1,0:T(8,128)(2,1)} %convolution_convert_fusion.3.q_ref.k_ref.v_ref, ...), custom_call_target="tpu_custom_call" | custom-call | flops 1073741824 | bytes 5242880 | tf_op jit(solution)/shard_map/conv/pallas_call | solution.py:91
  485.2 13.4 %share.4.all_ref = f32[16,16,512]{2,1,0:T(8,128)} custom-call(f32[16,512]{1,0:T(8,128)} %get-tuple-element.19.own_ref), custom_call_target="tpu_custom_call" | custom-call | bytes 5242880 | tf_op jit(solution)/shard_map/share/pallas_call | solution.py:150
  525.9 4.9 fusion.10
  530.8 8.8 %collective-permute-done.4 = bf16[512,512]{1,0:T(8,128)(2,1)S(1)} collective-permute-done((bf16[512,512]{1,0:T(8,128)(2,1)}, bf16[512,512]{1,0:T(8,128)(2,1)S(1)}, u32[]{:S(2)}, u32[]{:S(2)}) %collective-permute-start.4) | collective-permute-done | bytes 524320 | tf_op jit(solution)/shard_map/ppermute | solution.py:26
  544.5 6.2 %collective-permute-done.3 = bf16[512,512]{1,0:T(8,128)(2,1)S(1)} collective-permute-done((bf16[512,512]{1,0:T(8,128)(2,1)}, bf16[512,512]{1,0:T(8,128)(2,1)S(1)}, u32[]{:S(2)}, u32[]{:S(2)}) %collective-permute-start.3) | collective-permute-done | bytes 524320 | tf_op jit(solution)/shard_map/ppermute | solution.py:26
  550.7 4.9 fusion.8
  560.4 10.4 %add_convert_fusion = bf16[512,2048]{1,0:T(8,128)(2,1)} fusion(f32[512,2048]{1,0:T(8,128)S(1)} %fusion.2, f32[512,2048]{1,0:T(8,128)} %fusion.4, f32[512,2048]{1,0:T(8,128)S(1)} %fusion.6, f32[512,2048]{1,0:T(8,128)} %fusion.8, f32[512,2048]{1,0:T(8,128)} %fusion.10, f32[512,2048]{1,0:T(8,128)S(1)} %fusion.14, f32[512,2048]{1,0:T(8,128)} %fusion.12, ...), kind=kOutput, calls=%fused_computation.4 | convolution fusion | flops 1082130432 | bytes 34078720 | tf_op jit(solution)/shard_map/dot_general | solution.py:271
  (84 shorter events, 66.8 us)
Async XLA Ops:
  6.5 109.8 %all-gather.7.cloned.1.call-start = ((), (), s32[]{:S(2)}) async-start(), calls=%async_computation.1 | async-start | bytes 13369344 | tf_op jit(solution)/shard_map/all_gather | solution.py:217
  10.0 222.3 %all-gather.9.cloned.1.call-start = ((), (), s32[]{:S(2)}) async-start(), calls=%async_computation.2 | async-start | bytes 13369344 | tf_op jit(solution)/shard_map/all_gather | solution.py:217
  11.2 337.0 %all-gather.11.cloned.1.call-start = ((), (), s32[]{:S(2)}) async-start(), calls=%async_computation.3 | async-start | bytes 13369344 | tf_op jit(solution)/shard_map/all_gather | solution.py:217
  12.4 451.5 %all-gather.5.cloned.1.call-start = ((), (), s32[]{:S(2)}) async-start(), calls=%async_computation | async-start | bytes 13369344 | tf_op jit(solution)/shard_map/all_gather | solution.py:217
  14.6 95.2 %collective-permute-start = (bf16[2,4096]{1,0:T(2,128)(2,1)S(1)}, bf16[2,4096]{1,0:T(2,128)(2,1)S(1)}, u32[]{:S(2)}, u32[]{:S(2)}) collective-permute-start(bf16[2,4096]{1,0:T(2,128)(2,1)S(1)} %slice.139), channel_id=1, source_target_pairs={{0,2},{2,4},{4,6},{6,8},{8,10},{10,12},{12,14},{14,16},{16,18},{18... | collective-permute-start | bytes 49160 | tf_op jit(solution)/shard_map/ppermute | solution.py:21
  17.0 11.0 %copy-start.6 = (f32[128,16]{0,1:T(8,128)S(1)}, f32[128,16]{0,1:T(8,128)}, u32[]{:S(2)}) copy-start(f32[128,16]{0,1:T(8,128)} %param.10) | copy-start | bytes 24580
  17.0 11.0 %copy-start.7 = (f32[128,16]{0,1:T(8,128)S(1)}, f32[128,16]{0,1:T(8,128)}, u32[]{:S(2)}) copy-start(f32[128,16]{0,1:T(8,128)} %param.11) | copy-start | bytes 24580
  25.5 505.3 %collective-permute-start.2 = (bf16[2048,2048]{1,0:T(8,128)(2,1)}, bf16[2048,2048]{1,0:T(8,128)(2,1)}, u32[]{:S(2)}, u32[]{:S(2)}) collective-permute-start(bf16[2048,2048]{1,0:T(8,128)(2,1)} %constant_dynamic-slice_fusion), channel_id=1, source_target_pairs={{0,1},{1,0},{2,3},{3,2},{4,5},{5,4},{6,7},{7,6},{8,9},{9,8},{10,11... | collective-permute-start | bytes 25165832 | tf_op jit(solution)/shard_map/ppermute | solution.py:26
  88.0 6.9 %copy-start.5 = (f32[3,3,2048]{2,1,0:T(4,128)S(1)}, f32[3,3,2048]{2,1,0:T(4,128)}, u32[]{:S(2)}) copy-start(f32[3,3,2048]{2,1,0:T(4,128)} %param.9) | copy-start | bytes 221188
  95.9 3.2 copy-start
  103.5 2.2 copy-start.8
  502.2 53.4 %collective-permute-start.1 = (bf16[512,512]{1,0:T(8,128)(2,1)}, bf16[512,512]{1,0:T(8,128)(2,1)S(1)}, u32[]{:S(2)}, u32[]{:S(2)}) collective-permute-start(bf16[512,512]{1,0:T(8,128)(2,1)} %mix.4), channel_id=1, source_target_pairs={{0,1},{1,0},{2,3},{3,2},{4,5},{5,4},{6,7},{7,6},{8,9},{9,8},{10,11... | collective-permute-start | bytes 1572872 | tf_op jit(solution)/shard_map/ppermute | solution.py:26
  507.2 53.2 %collective-permute-start.5 = (bf16[512,512]{1,0:T(8,128)(2,1)}, bf16[512,512]{1,0:T(8,128)(2,1)S(1)}, u32[]{:S(2)}, u32[]{:S(2)}) collective-permute-start(bf16[512,512]{1,0:T(8,128)(2,1)} %mix.7), channel_id=1, source_target_pairs={{0,1},{1,0},{2,3},{3,2},{4,5},{5,4},{6,7},{7,6},{8,9},{9,8},{10,11... | collective-permute-start | bytes 1572872 | tf_op jit(solution)/shard_map/ppermute | solution.py:26
  507.7 9.4 %copy-start.4 = (bf16[512,512]{1,0:T(8,128)(2,1)S(1)}, bf16[512,512]{1,0:T(8,128)(2,1)}, u32[]{:S(2)}) copy-start(bf16[512,512]{1,0:T(8,128)(2,1)} %mix.4) | copy-start | bytes 1572868
  511.3 28.4 %collective-permute-start.4 = (bf16[512,512]{1,0:T(8,128)(2,1)}, bf16[512,512]{1,0:T(8,128)(2,1)S(1)}, u32[]{:S(2)}, u32[]{:S(2)}) collective-permute-start(bf16[512,512]{1,0:T(8,128)(2,1)} %mix.6), channel_id=1, source_target_pairs={{0,1},{1,0},{2,3},{3,2},{4,5},{5,4},{6,7},{7,6},{8,9},{9,8},{10,11... | collective-permute-start | bytes 1572872 | tf_op jit(solution)/shard_map/ppermute | solution.py:26
  516.5 3.5 copy-start.1
  516.5 34.2 %collective-permute-start.3 = (bf16[512,512]{1,0:T(8,128)(2,1)}, bf16[512,512]{1,0:T(8,128)(2,1)S(1)}, u32[]{:S(2)}, u32[]{:S(2)}) collective-permute-start(bf16[512,512]{1,0:T(8,128)(2,1)} %mix.5), channel_id=1, source_target_pairs={{0,1},{1,0},{2,3},{3,2},{4,5},{5,4},{6,7},{7,6},{8,9},{9,8},{10,11... | collective-permute-start | bytes 1572872 | tf_op jit(solution)/shard_map/ppermute | solution.py:26
  520.0 3.0 copy-start.2
  523.0 3.0 copy-start.3
Sparse Core Ops, SparseCore 0:
  10.1 106.2 all-gather.6
  118.5 113.7 all-gather.8
  234.4 113.7 all-gather.10
  350.2 113.6 all-gather.4

commit v2 on v1

v2 whole, which is shorter than its diff:
```python
import functools

import jax
import jax.numpy as jnp
from jax import lax
from jax.experimental import pallas as pl
from jax.experimental.pallas import tpu as pltpu
from jax.sharding import PartitionSpec as P

SUB = 128
LANES = 256
HALO = 16
MESH = pl.DeviceIdType.MESH
HIGHEST = lax.Precision.HIGHEST


def shifted_by(block, axis, distance):
    devices = range(lax.axis_size(axis))
    route = [(i - distance, i) for i in devices if i - distance in devices]
    return lax.ppermute(block, axis, route)


def rotated(block, axis, distance):
    size = lax.axis_size(axis)
    return lax.ppermute(block, axis, [(i, (i + distance) % size) for i in range(size)])


def fanned(state, width, order):
    lanes = state.shape[1]
    tile = lanes // width
    full = jnp.concatenate([state] * tile, axis=0)
    row = lax.broadcasted_iota(jnp.int32, full.shape, 0) // order
    lane = lax.broadcasted_iota(jnp.int32, full.shape, 1) // width
    return jnp.where(row == lane, full, 0.0)


def conv_kernel(
    width, q_ref, k_ref, v_ref, taps_ref, toep_ref, leave_ref, reach_ref, fade_ref, skip_ref,
    query_ref, base_ref, state_ref
):
    taps = taps_ref.shape[0]
    count, lanes = query_ref.shape
    order = state_ref.shape[0]
    tile = lanes // width

    def filtered(ref, which):
        value = ref[...].astype(jnp.float32)
        total = None
        for tap in range(taps):
            term = taps_ref[tap, which][None, :] * value[HALO - tap : HALO - tap + count]
            total = term if total is None else total + term
        return total

    query_ref[...] = filtered(q_ref, 0)
    gated = filtered(k_ref, 1) * filtered(v_ref, 2)
    lane = lax.broadcasted_iota(jnp.int32, (SUB, lanes), 1) // width
    row = lax.broadcasted_iota(jnp.int32, (tile * order, lanes), 0) // order
    diagonal = row == lax.broadcasted_iota(jnp.int32, (tile * order, lanes), 1) // width
    toep = toep_ref[...].reshape(tile * SUB, SUB)
    state = jnp.zeros((tile * order, lanes), jnp.float32)
    for block in range(count // SUB):
        piece = gated[block * SUB : (block + 1) * SUB]
        wide = jnp.dot(toep, piece.astype(jnp.bfloat16), preferred_element_type=jnp.float32)
        local = skip_ref[...] * piece
        picked = wide[:SUB]
        for g in range(1, tile):
            picked = jnp.where(lane == g, wide[g * SUB : (g + 1) * SUB], picked)
        local = local + picked
        if block:
            local = local + jnp.dot(
                reach_ref[:SUB], state, precision=HIGHEST, preferred_element_type=jnp.float32
            )
        base_ref[block * SUB : (block + 1) * SUB] = local
        fresh = jnp.dot(
            leave_ref[...], piece, precision=HIGHEST, preferred_element_type=jnp.float32
        )
        state = fade_ref[...] * state + jnp.where(diagonal, fresh, 0.0)
    compact = state[:order]
    for g in range(1, tile):
        compact = compact + state[g * order : (g + 1) * order]
    state_ref[...] = compact


def convolved(proj, taps, toep, leave, reach, fade, skip, width, order, count):
    chans = skip.shape[1]
    lanes = min(LANES, chans)
    steps = chans // lanes
    tile = lanes // width
    segments, rows, _ = proj.shape
    return pl.pallas_call(
        functools.partial(conv_kernel, width),
        grid=(steps, segments),
        in_specs=[
            pl.BlockSpec((None, rows, lanes), lambda i, j: (j, 0, i)),
            pl.BlockSpec((None, rows, lanes), lambda i, j: (j, 0, steps + i)),
            pl.BlockSpec((None, rows, lanes), lambda i, j: (j, 0, 2 * steps + i)),
            pl.BlockSpec((taps.shape[0], 3, lanes), lambda i, j: (0, 0, i)),
            pl.BlockSpec((tile, SUB, SUB), lambda i, j: (i, 0, 0)),
            pl.BlockSpec((tile * order, SUB), lambda i, j: (i, 0)),
            pl.BlockSpec((count, tile * order), lambda i, j: (0, i)),
            pl.BlockSpec((tile * order, 1), lambda i, j: (i, 0)),
            pl.BlockSpec((1, lanes), lambda i, j: (0, i)),
        ],
        out_specs=[
            pl.BlockSpec((None, count, lanes), lambda i, j: (j, 0, i)),
            pl.BlockSpec((None, count, lanes), lambda i, j: (j, 0, i)),
            pl.BlockSpec((None, order, lanes), lambda i, j: (j, 0, i)),
        ],
        out_shape=[
            jax.ShapeDtypeStruct((segments, count, chans), jnp.float32),
            jax.ShapeDtypeStruct((segments, count, chans), jnp.float32),
            jax.ShapeDtypeStruct((segments, order, chans), jnp.float32),
        ],
        cost_estimate=pl.CostEstimate(
            flops=2 * count * chans * SUB * tile, bytes_accessed=count * chans * 20, transcendentals=0
        ),
        name="conv",
    )(proj, proj, proj, taps, toep, leave, reach, fade, skip)


def place():
    size, here = lax.axis_size("seq"), lax.axis_index("seq")
    return here // 4, lax.rem(here // 2, 2), lax.rem(here, 2), size // 4


def index_of(z, x, core):
    return z * 4 + x * 2 + core


def greet(peers):
    barrier = pltpu.get_barrier_semaphore()
    for peer in peers:
        pl.semaphore_signal(barrier, inc=1, device_id=peer, device_id_type=MESH)
    pl.semaphore_wait(barrier, len(peers))


def remote(source, target, send_sem, recv_sem, peer):
    return pltpu.make_async_remote_copy(
        src_ref=source,
        dst_ref=target,
        send_sem=send_sem,
        recv_sem=recv_sem,
        device_id=peer,
        device_id_type=MESH,
    )


def gather_kernel(
    own_ref, pieces_ref, tok_ref, w_ref, local_sems,
    line_send, line_recv, pass_send, pass_recv, pair_send, pair_recv,
    tp_send, tp_recv, core_send, core_recv, early_send, early_recv,
):
    z, x, core, depth = place()
    parity = lax.rem(z, 2)
    mate = z + 1 - 2 * parity
    n_tp, part = lax.axis_size("tp"), lax.axis_index("tp")
    cols = own_ref.shape[1] // n_tp
    mine = index_of(z, x, core)
    side = {"seq": index_of(z, 1 - x, core)}
    twin = {"seq": index_of(z, x, 1 - core)}
    pair = {"seq": index_of(mate, x, core)}

    def on_line(step, other, sign):
        there = lax.rem(z + sign * step + depth, depth)
        return there, (1 - core if other else core)

    hops = [(step, other) for step in range(depth) for other in range(2)][1:]
    hops = sorted(hops, key=lambda hop: (min(hop[0], depth - hop[0]), hop))
    peers = [side]
    for hop in hops:
        there, which = on_line(*hop, 1)
        peers.append({"seq": index_of(there, x, which)})
    tps = [{"tp": lax.rem(part + d, n_tp)} for d in range(1, n_tp)]
    greet(peers + tps)

    def band(which):
        return pl.ds(pl.multiple_of(which * cols, cols), cols)

    own_slot, mate_slot = 2 * parity + core, 2 * (1 - parity) + core
    role = own_slot
    stay = [
        pltpu.make_async_copy(own_ref, tok_ref.at[own_slot], local_sems.at[0]),
        pltpu.make_async_copy(pieces_ref.at[role], w_ref.at[mine], local_sems.at[1]),
    ]
    for copy in stay:
        copy.start()
    started = []

    def begin(copy):
        copy.start()
        started.append(copy)
        return copy

    first = begin(remote(
        pieces_ref.at[role], w_ref.at[mine], pass_send.at[0], pass_recv.at[0], side
    ))
    line = {}
    paired = None
    for n, hop in enumerate(hops):
        if n == 4 or (n == len(hops) - 1 and paired is None):
            paired = begin(remote(
                own_ref.at[:, band(part)], tok_ref.at[own_slot, :, band(part)],
                pair_send, pair_recv, pair,
            ))
        there, which = on_line(*hop, 1)
        index = 2 * hop[0] + hop[1]
        line[hop] = begin(remote(
            pieces_ref.at[2 * lax.rem(there, 2) + which], w_ref.at[mine],
            line_send.at[index], line_recv.at[index], {"seq": index_of(there, x, which)},
        ))
    early = begin(remote(own_ref, tok_ref.at[own_slot], early_send, early_recv, twin))

    forwards = []

    def hand_on(hop):
        index = 2 * hop[0] + hop[1]
        there, which = on_line(*hop, -1)
        source = index_of(there, x, which)
        line[hop].wait_recv()
        forwards.append(begin(remote(
            w_ref.at[source], w_ref.at[source], pass_send.at[index], pass_recv.at[index], side
        )))

    def to_twin(which, slot):
        return begin(remote(
            tok_ref.at[mate_slot, :, band(which)], tok_ref.at[mate_slot, :, band(which)],
            core_send.at[slot], core_recv.at[slot], twin,
        ))

    for hop in hops[:4]:
        hand_on(hop)
    paired.wait_recv()
    across = []
    for d in range(1, n_tp):
        across.append(begin(remote(
            tok_ref.at[mate_slot, :, band(part)], tok_ref.at[mate_slot, :, band(part)],
            tp_send.at[d - 1], tp_recv.at[d - 1], tps[d - 1],
        )))
    twins = [to_twin(part, 0)]
    for hop in hops[4:]:
        hand_on(hop)
    for d in range(1, n_tp):
        across[d - 1].wait_recv()
        twins.append(to_twin(lax.rem(part - d + n_tp, n_tp), d))
    for copy in [first, early] + forwards + twins:
        copy.wait_recv()
    for copy in started:
        copy.wait_send()
    for copy in stay:
        copy.wait()


def gathered(own, pieces):
    size, n_tp = lax.axis_size("seq"), lax.axis_size("tp")
    line = size // 2
    anywhere = pl.BlockSpec(memory_space=pl.ANY)
    one = pltpu.SemaphoreType.DMA(())
    return pl.pallas_call(
        gather_kernel,
        out_shape=[
            jax.ShapeDtypeStruct((4,) + own.shape, own.dtype),
            jax.ShapeDtypeStruct((size,) + pieces.shape[1:], pieces.dtype),
        ],
        in_specs=[anywhere, anywhere],
        out_specs=[anywhere, anywhere],
        scratch_shapes=[
            pltpu.SemaphoreType.DMA((2,)),
            pltpu.SemaphoreType.DMA((line,)),
            pltpu.SemaphoreType.DMA((line,)),
            pltpu.SemaphoreType.DMA((line,)),
            pltpu.SemaphoreType.DMA((line,)),
            one,
            one,
            pltpu.SemaphoreType.DMA((n_tp,)),
            pltpu.SemaphoreType.DMA((n_tp,)),
            pltpu.SemaphoreType.DMA((n_tp,)),
            pltpu.SemaphoreType.DMA((n_tp,)),
            one,
            one,
        ],
        compiler_params=pltpu.CompilerParams(collective_id=0, has_side_effects=True),
        name="gather",
    )(own, pieces)


def share_kernel(own_ref, all_ref, send_sems, recv_sems):
    total = all_ref.shape[0]
    z, x, core, depth = place()
    here = (z // 2) * 2 + x

    def peer(d):
        there = lax.rem(here + d, total)
        return {"seq": index_of(2 * (there // 2) + lax.rem(z, 2), lax.rem(there, 2), core)}

    peers = [peer(d) for d in range(1, total)]
    greet(peers)
    copies = []
    for d in range(1, total):
        copy = remote(
            own_ref, all_ref.at[here], send_sems.at[d - 1], recv_sems.at[d - 1], peers[d - 1]
        )
        copy.start()
        copies.append(copy)
    all_ref[here] = own_ref[...]
    for copy in copies:
        copy.wait()


def shared(state):
    total = lax.axis_size("seq") // 4
    return pl.pallas_call(
        share_kernel,
        out_shape=jax.ShapeDtypeStruct((total,) + state.shape, state.dtype),
        in_specs=[pl.BlockSpec(memory_space=pltpu.VMEM)],
        out_specs=pl.BlockSpec(memory_space=pltpu.VMEM),
        scratch_shapes=[
            pltpu.SemaphoreType.DMA((total - 1,)),
            pltpu.SemaphoreType.DMA((total - 1,)),
        ],
        compiler_params=pltpu.CompilerParams(collective_id=1, has_side_effects=True),
        name="share",
    )(state)


def spread_kernel(mix_ref, full_ref, local_sem, send_sems, recv_sems):
    z, x, core, _ = place()
    parity = lax.rem(z, 2)
    me = 2 * parity + core
    base = 2 * (z // 2)

    def peer(d):
        there = lax.rem(me + d, 4)
        return there, {"seq": index_of(base + there // 2, x, lax.rem(there, 2))}

    greet([peer(d)[1] for d in range(1, 4)])
    copies = []
    for d in (2, 1, 3):
        there, device = peer(d)
        copy = remote(
            mix_ref.at[there], full_ref.at[me], send_sems.at[d - 1], recv_sems.at[d - 1], device
        )
        copy.start()
        copies.append(copy)
    stay = pltpu.make_async_copy(mix_ref.at[me], full_ref.at[me], local_sem)
    stay.start()
    for copy in copies:
        copy.wait()
    stay.wait()


def spread(mix):
    return pl.pallas_call(
        spread_kernel,
        out_shape=jax.ShapeDtypeStruct(mix.shape, mix.dtype),
        in_specs=[pl.BlockSpec(memory_space=pltpu.VMEM)],
        out_specs=pl.BlockSpec(memory_space=pltpu.VMEM),
        scratch_shapes=[
            pltpu.SemaphoreType.DMA(()),
            pltpu.SemaphoreType.DMA((3,)),
            pltpu.SemaphoreType.DMA((3,)),
        ],
        compiler_params=pltpu.CompilerParams(collective_id=2, has_side_effects=True),
        name="spread",
    )(mix)


def mix_kernel(width, query_ref, base_ref, all_ref, weight_ref, reach_ref, mix_ref):
    order = all_ref.shape[1]
    entering = jnp.sum(all_ref[...] * weight_ref[...], axis=0)
    carried = jnp.dot(
        reach_ref[...],
        fanned(entering, width, order),
        precision=HIGHEST,
        preferred_element_type=jnp.float32,
    )
    mix_ref[...] = (query_ref[...] * (base_ref[...] + carried)).astype(mix_ref.dtype)


def mixed_of(query, base, everything, weight, reach, width):
    segments, count, chans = query.shape
    size, order, _ = everything.shape
    lanes = min(LANES, chans)
    cols = lanes // width * order
    return pl.pallas_call(
        functools.partial(mix_kernel, width),
        grid=(chans // lanes, segments),
        in_specs=[
            pl.BlockSpec((None, count, lanes), lambda i, j: (j, 0, i)),
            pl.BlockSpec((None, count, lanes), lambda i, j: (j, 0, i)),
            pl.BlockSpec((size, order, lanes), lambda i, j: (0, 0, i)),
            pl.BlockSpec((None, size, order, lanes), lambda i, j: (j, 0, 0, i)),
            pl.BlockSpec((count, cols), lambda i, j: (0, i)),
        ],
        out_specs=pl.BlockSpec((None, count, lanes), lambda i, j: (j, 0, i)),
        out_shape=jax.ShapeDtypeStruct((segments, count, chans), jnp.bfloat16),
        name="mix",
    )(query, base, everything, weight, reach)


def shards(tokens, w_in, short_taps, decay_rate, residue, skip_gain, w_out):
    count = tokens.shape[0]
    rows, _, all_chans = w_in.shape
    width = all_chans // decay_rate.shape[0]
    taps = short_taps.shape[0]
    z, x, core, depth = place()
    parity = lax.rem(z, 2)
    role = 2 * parity + core
    n_tp, part = lax.axis_size("tp"), lax.axis_index("tp")
    chans = all_chans // 4

    before = shifted_by(tokens[count - (taps - 1) :], "seq", 1)
    extended = jnp.concatenate(
        [jnp.zeros((HALO - (taps - 1), tokens.shape[1]), tokens.dtype), before, tokens], axis=0
    )
    pieces = w_in.reshape(rows, 3, 4, chans).transpose(2, 0, 1, 3).reshape(4, rows, 3 * chans)
    tok, weights = gathered(extended, pieces)

    def own(array, axis):
        share = array.shape[axis] // 4
        return lax.dynamic_slice_in_dim(array, role * share, share, axis)

    short_taps, skip = own(short_taps, 2), own(skip_gain[None], 1)
    decay_rate, residue = own(decay_rate, 0), own(residue, 0)
    groups, order = decay_rate.shape
    weight_mode = residue * jnp.sqrt(2.0 * decay_rate / order)
    offsets = jnp.arange(SUB, dtype=jnp.float32)
    kernel = jnp.einsum(
        "gm,gmd->gd",
        weight_mode,
        jnp.exp(-decay_rate[:, :, None] * offsets[None, None, :]),
        precision=HIGHEST,
    )
    lag = jnp.arange(SUB)[:, None] - jnp.arange(SUB)[None, :]
    toep = jnp.where(lag[None] >= 0, kernel[:, jnp.maximum(lag, 0)], 0.0).astype(jnp.bfloat16)
    rate = decay_rate.reshape(groups * order)
    leave = jnp.exp(-rate[:, None] * (SUB - 1.0 - offsets[None, :]))
    fade = jnp.exp(-rate * SUB)[:, None]
    positions = jnp.arange(count, dtype=jnp.float32)
    reach = weight_mode.reshape(groups * order)[None] * jnp.exp(
        -rate[None] * (positions[:, None] + 1.0)
    )
    by_mode = jnp.repeat(decay_rate.T, width, axis=1)
    slot = jnp.arange(4)
    own_block = index_of(2 * (z // 2) + slot // 2, x, slot % 2)
    team = jnp.arange(depth)[:, None]
    other_block = index_of(2 * (team // 2) + slot[None] // 2, team % 2, slot[None] % 2).reshape(-1)
    ahead = (own_block[:, None] - 1 - other_block[None, :])[:, :, None, None]
    weight = jnp.where(
        ahead >= 0, jnp.exp(-by_mode * (count * jnp.maximum(ahead, 0).astype(jnp.float32))), 0.0
    )

    proj = jnp.dot(
        tok.reshape(-1, tok.shape[2]),
        weights.reshape(-1, weights.shape[2]),
        preferred_element_type=jnp.float32,
    ).astype(jnp.bfloat16).reshape(4, -1, 3 * chans)
    query, base, final = convolved(
        proj, short_taps, toep, leave, reach, fade, skip, width, order, count
    )
    everything = shared(final).reshape(-1, order, chans)
    mix = spread(mixed_of(query, base, everything, weight, reach, width))
    full = mix.transpose(1, 0, 2).reshape(count, 4 * chans)

    share = w_out.shape[1] // n_tp
    half = share // 2

    def product(target, piece):
        cols = lax.dynamic_slice_in_dim(w_out, target * share + piece * half, half, axis=1)
        return jnp.dot(full, cols, preferred_element_type=jnp.float32).astype(jnp.bfloat16)

    arrived = []
    for d in range(1, n_tp):
        for piece in range(2):
            arrived.append(rotated(product((part + d) % n_tp, piece), "tp", d))
    results = []
    for piece in range(2):
        total = product(part, piece).astype(jnp.float32)
        for d in range(1, n_tp):
            total = total + arrived[2 * (d - 1) + piece].astype(jnp.float32)
        results.append(total.astype(jnp.bfloat16))
    return jnp.concatenate(results, axis=1)


def solution(mesh):
    in_specs = (
        P("seq", None),
        P("seq", None, "tp"),
        P(None, None, "tp"),
        P("tp", None),
        P("tp", None),
        P("tp"),
        P("tp", None),
    )
    out_specs = P("seq", "tp")
    return jax.shard_map(shards, mesh=mesh, in_specs=in_specs, out_specs=out_specs, check_vma=False)
```

time: 583 us -> 477 us (0.82)
  waiting for transfers between devices: 243 us -> 35.7 us
  Pallas kernels: 127 us -> 290 us
  matrix products: 86.9 us -> 54.3 us
  local copies, waits for them, and re-layouts: 94.2 us -> 76.9 us
  between operations: 13.7 us -> 0.23 us
  other arithmetic: 3.78 us -> 14.2 us
    all_gather x4 -> x0, waiting for transfers between devices: 228 us -> none  [shards(): pieces.append(lax.all_gather(cols, 'seq', axis=0, tiled=True))]
    pallas_call x8 -> x4, Pallas kernels: 112 us -> 281 us  [the longest x1 208 us: gathered(): pl.pallas_call(gather_kernel, out_shape=[jax.ShapeDtypeStruct((4,) + own....]
    dot_general x12 -> x5, matrix products: 86.9 us -> 54.3 us  [the longest x1 34.5 us: shards(): jnp.dot(tok.reshape(-1, tok.shape[2]), weights.reshape(-1, weights.shape[...]
    ppermute x5 -> x2, waiting for transfers between devices: 15 us -> 35.6 us  [rotated(): lax.ppermute(block, axis, [(i, (i + distance) % size) for i in range(size)])]
    slice x12 -> x0, local copies, waits for them, and re-layouts: 13.7 us -> none  [the longest x5 3.42 us: shards(): fade[mode]]
    concatenate x0 -> x2, other arithmetic: none -> 7.9 us  [the longest x1 6.4 us: shards(): jnp.concatenate([jnp.zeros((HALO - (taps - 1), tokens.shape[1]), tokens.d...]
    dynamic_slice x1, local copies, waits for them, and re-layouts: 8.46 us -> 0.61 us  [own(): return lax.dynamic_slice_in_dim(array, role * share, share, axis)]
    pallas_call x4 -> x1, Pallas kernels: 14.4 us -> 9.93 us  [mixed_of(): pl.pallas_call(functools.partial(mix_kernel, width), grid=(chans // lanes...]
  transfers between devices with their start and end apart: 10 -> 3, of which waited for: 6 -> 2; matrix products, arithmetic and copies ran while one was open for 30% -> 19% of each run, Pallas kernels for 22% -> 0%
where the time goes in v2:
time: 477 us; the launch traced here: 476 us
  Pallas kernels  290 us (61%)
  local copies, waits for them, and re-layouts  76.9 us (16%)
  matrix products  54.3 us (11%)
  waiting for transfers between devices  35.7 us (7%)
  other arithmetic  14.2 us (3%)
    pallas_call x1, Pallas kernels, gathered(): pl.pallas_call(gather_kernel, out_shape=[jax.ShapeDtypeStruct((4,) + own....  208 us
    gather x2, local copies, waits for them, and re-layouts, shards(): kernel[:, jnp.maximum(lag, 0)]  61.8 us
    ppermute x2, waiting for transfers between devices, rotated(): lax.ppermute(block, axis, [(i, (i + distance) % size) for i in range(size)])  35.6 us
    dot_general x1, matrix products, shards(): jnp.dot(tok.reshape(-1, tok.shape[2]), weights.reshape(-1, weights.shape[...  34.5 us
    pallas_call x1, Pallas kernels, convolved(): pl.pallas_call(functools.partial(conv_kernel, width), grid=(steps, segmen...  30.1 us
    pallas_call x1, Pallas kernels, spread(): pl.pallas_call(spread_kernel, out_shape=jax.ShapeDtypeStruct(mix.shape, m...  27.9 us
    dot_general x4, matrix products, product(): jnp.dot(full, cols, preferred_element_type=jnp.float32).astype(jnp.bfloat16)  19.8 us
    pallas_call x1, Pallas kernels, shared(): pl.pallas_call(share_kernel, out_shape=jax.ShapeDtypeStruct((total,) + st...  14.6 us
  transfers between devices with their start and end apart: 3, of which 2 were waited for; matrix products, arithmetic and copies ran while one was open for 19% of the time, Pallas kernels for 0%

profile of v2, /device:TPU:0, one launch (start us, length us, event | category | flops | bytes accessed | tf_op | source)
XLA Modules:
  0.0 476.2 jit_solution(4792109428160986195)
XLA Ops:
  0.9 2.4 collective-permute-start
  5.3 57.8 %gather_fusion = bf16[16384,32]{1,0:T(8,128)(2,1)} fusion(bf16[32,128]{0,1:T(8,128)(2,1)S(1)} %copy.33, s32[16384]{0:T(1024)S(1)} %bitcast_clamp_fusion), kind=kCustom, calls=%fused_computation | custom fusion | bytes 2162688 | tf_op jit(solution)/shard_map/gather | solution.py:434
  63.1 4.0 copy.34
  67.4 1.3 fusion.24.toep_ref
  70.7 1.7 exponential_select_fusion.weight_ref
  73.0 2.8 copy.20
  75.8 2.1 copy.21
  77.9 2.8 copy.22.pieces_ref
  83.0 6.4 %pad_maximum_fusion.own_ref = bf16[528,4096]{1,0:T(8,128)(2,1)} fusion(bf16[512,4096]{1,0:T(8,128)(2,1)} %param.7, bf16[2,4096]{1,0:T(2,128)(2,1)S(1)} %collective-permute-done, bf16[528]{0:T(1024)(128)(2,1)S(1)} %pad.2.clone), kind=kLoop, calls=%fused_computation.2 | loop fusion | flops 12976128 | bytes 8537120 | tf_op jit(solution)/shard_map/concatenate | solution.py:412
  89.4 208.0 %gather.7 = (bf16[4,528,4096]{2,1,0:T(8,128)(2,1)}, bf16[16,256,1536]{2,1,0:T(8,128)(2,1)}) custom-call(bf16[528,4096]{1,0:T(8,128)(2,1)} %pad_maximum_fusion.own_ref, bf16[4,256,1536]{2,1,0:T(8,128)(2,1)} %copy.22.pieces_ref), custom_call_target="tpu_custom_call" | custom-call | tf_op jit(solution)/shard_map/gather/pallas_call | solution.py:258
  297.3 34.5 %convolution_convert_fusion = bf16[2112,1536]{1,0:T(8,128)(2,1)} fusion(bf16[2112,4096]{1,0:T(8,128)(2,1)} %bitcast.37, bf16[4096,1536]{1,0:T(8,128)(2,1)} %bitcast.38), kind=kOutput, calls=%fused_computation.1 | convolution fusion | flops 26578354176 | bytes 36372480 | tf_op jit(solution)/shard_map/dot_general | solution.py:452
  331.8 30.1 %conv.1 = (f32[4,512,512]{2,1,0:T(8,128)}, f32[4,512,512]{2,1,0:T(8,128)}, f32[4,16,512]{2,1,0:T(8,128)}) custom-call(bf16[4,528,1536]{2,1,0:T(8,128)(2,1)} %bitcast.23, bf16[4,528,1536]{2,1,0:T(8,128)(2,1)} %bitcast.24, bf16[4,528,1536]{2,1,0:T(8,128)(2,1)} %bitcast.25, f32[3,3,512]{2,1,0:T(4,128)} %constant_dynamic-slice_fusion.taps_ref, ...), custom_call_target="tpu_custom_call" | custom-call | flops 1073741824 | bytes 5242880 | tf_op jit(solution)/shard_map/conv/pallas_call | solution.py:90
  362.0 14.6 %share.1 = f32[4,4,16,512]{3,2,1,0:T(8,128)} custom-call(f32[4,16,512]{2,1,0:T(8,128)} %get-tuple-element.14.own_ref), custom_call_target="tpu_custom_call" | custom-call | tf_op jit(solution)/shard_map/share/pallas_call | solution.py:311
  376.5 9.9 %mix.1.mix_ref = bf16[4,512,512]{2,1,0:T(8,128)(2,1)} custom-call(f32[4,512,512]{2,1,0:T(8,128)} %get-tuple-element.12.query_ref, f32[4,512,512]{2,1,0:T(8,128)} %get-tuple-element.13.base_ref, f32[16,16,512]{2,1,0:T(8,128)} %bitcast.30, f32[4,16,16,512]{3,2,1,0:T(8,128)} %exponential_select_fusion.weight_ref, f32[512,512]{1,0:T(8,128)} %exponential_multiply_fusion.reach_ref), custom_call_target="tpu_custom_call" | custom-call | tf_op jit(solution)/shard_map/mix/pallas_call | solution.py:384
  386.5 27.9 %spread.1 = bf16[4,512,512]{2,1,0:T(8,128)(2,1)} custom-call(bf16[4,512,512]{2,1,0:T(8,128)(2,1)} %mix.1.mix_ref), custom_call_target="tpu_custom_call" | custom-call | tf_op jit(solution)/shard_map/spread/pallas_call | solution.py:352
  414.3 2.8 copy.29
  417.1 4.5 fusion.17
  421.7 1.3 collective-permute-start.2
  423.0 5.5 %fusion.11 = bf16[512,1024]{1,0:T(8,128)(2,1)} fusion(bf16[512,2048]{0,1:T(8,128)(2,1)S(1)} %bitcast.32, bf16[2048,4096]{1,0:T(8,128)(2,1)} %param.13, s32[]{:T(128)S(6)} %select_n.114), kind=kOutput, calls=%fused_computation.17 | convolution fusion | flops 2148007936 | bytes 7340036 | tf_op jit(solution)/shard_map/dot_general | solution.py:469
  429.3 18.6 %collective-permute-done.2 = bf16[512,1024]{1,0:T(8,128)(2,1)} collective-permute-done((bf16[512,1024]{1,0:T(8,128)(2,1)S(1)}, bf16[512,1024]{1,0:T(8,128)(2,1)}, u32[]{:S(2)}, u32[]{:S(2)}) %collective-permute-start.2) | collective-permute-done | bytes 1048608 | tf_op jit(solution)/shard_map/ppermute | solution.py:25
  447.9 4.8 %add_convert_fusion = bf16[512,1024]{1,0:T(8,128)(2,1)S(1)} fusion(bf16[512,1024]{1,0:T(8,128)(2,1)} %collective-permute-done.2, bf16[512,2048]{0,1:T(8,128)(2,1)S(1)} %bitcast.33, bf16[2048,4096]{1,0:T(8,128)(2,1)} %param.13, s32[]{:T(128)S(6)} %select_n.115), kind=kOutput, calls=%fused_computation.13 | convolution fusion | flops 2150105088 | bytes 8388612 | tf_op jit(solution)/shard_map/dot_general | solution.py:469
  452.7 17.0 %collective-permute-done.1 = bf16[512,1024]{1,0:T(8,128)(2,1)} collective-permute-done((bf16[512,1024]{1,0:T(8,128)(2,1)}, bf16[512,1024]{1,0:T(8,128)(2,1)}, u32[]{:S(2)}, u32[]{:S(2)}) %collective-permute-start.1) | collective-permute-done | bytes 1048608 | tf_op jit(solution)/shard_map/ppermute | solution.py:25
  469.8 4.9 %add_convert_fusion.1 = bf16[512,1024]{1,0:T(8,128)(2,1)S(1)} fusion(bf16[512,1024]{1,0:T(8,128)(2,1)} %collective-permute-done.1, bf16[512,2048]{0,1:T(8,128)(2,1)S(1)} %bitcast.34, bf16[2048,4096]{1,0:T(8,128)(2,1)} %param.13, s32[]{:T(128)S(6)} %select_n.112), kind=kOutput, calls=%fused_computation.14 | convolution fusion | flops 2150105088 | bytes 8388612 | tf_op jit(solution)/shard_map/dot_general | solution.py:469
  474.7 1.5 pad_maximum_fusion.1
  (37 shorter events, 8.6 us)
Async XLA Ops:
  0.0 72.4 %copy-start = (f32[3,3,2048]{2,1,0:T(4,128)S(1)}, f32[3,3,2048]{2,1,0:T(4,128)}, u32[]{:S(2)}) copy-start(f32[3,3,2048]{2,1,0:T(4,128)} %param.9) | copy-start | bytes 221188
  0.9 82.1 %collective-permute-start = (bf16[2,4096]{1,0:T(2,128)(2,1)S(1)}, bf16[2,4096]{1,0:T(2,128)(2,1)S(1)}, u32[]{:S(2)}, u32[]{:S(2)}) collective-permute-start(bf16[2,4096]{1,0:T(2,128)(2,1)S(1)} %slice.3), channel_id=1, source_target_pairs={{0,2},{2,4},{4,6},{6,8},{8,10},{10,12},{12,14},{14,16},{16,18},{18... | collective-permute-start | bytes 49160 | tf_op jit(solution)/shard_map/ppermute | solution.py:20
  68.7 4.3 copy-start.2
  421.7 26.2 %collective-permute-start.2 = (bf16[512,1024]{1,0:T(8,128)(2,1)S(1)}, bf16[512,1024]{1,0:T(8,128)(2,1)}, u32[]{:S(2)}, u32[]{:S(2)}) collective-permute-start(bf16[512,1024]{1,0:T(8,128)(2,1)S(1)} %fusion.17), channel_id=1, source_target_pairs={{0,1},{1,0},{2,3},{3,2},{4,5},{5,4},{6,7},{7,6},{8,9},{9,8},{10,11... | collective-permute-start | bytes 3145736 | tf_op jit(solution)/shard_map/ppermute | solution.py:25
  428.5 41.2 %collective-permute-start.1 = (bf16[512,1024]{1,0:T(8,128)(2,1)}, bf16[512,1024]{1,0:T(8,128)(2,1)}, u32[]{:S(2)}, u32[]{:S(2)}) collective-permute-start(bf16[512,1024]{1,0:T(8,128)(2,1)} %fusion.11), channel_id=1, source_target_pairs={{0,1},{1,0},{2,3},{3,2},{4,5},{5,4},{6,7},{7,6},{8,9},{9,8},{10,11... | collective-permute-start | bytes 3145736 | tf_op jit(solution)/shard_map/ppermute | solution.py:25
  469.8 6.4 %copy-start.1 = (f32[3,3,2048]{2,1,0:T(4,128)S(1)}, f32[3,3,2048]{2,1,0:T(4,128)}, u32[]{:S(2)}) copy-start(f32[3,3,2048]{2,1,0:T(4,128)} %param.9) | copy-start | bytes 221188

commit v3 on v2

--- a/solution.py
+++ b/solution.py
@@ -18,11 +18,6 @@
     devices = range(lax.axis_size(axis))
     route = [(i - distance, i) for i in devices if i - distance in devices]
     return lax.ppermute(block, axis, route)
-
-
-def rotated(block, axis, distance):
-    size = lax.axis_size(axis)
-    return lax.ppermute(block, axis, [(i, (i + distance) % size) for i in range(size)])
 
 
 def fanned(state, width, order):
@@ -34,9 +29,20 @@
     return jnp.where(row == lane, full, 0.0)
 
 
+def split(value):
+    high = value.astype(jnp.bfloat16)
+    return high, (value - high.astype(jnp.float32)).astype(jnp.bfloat16)
+
+
+def product3(a, b):
+    (ah, al), (bh, bl) = split(a), split(b)
+    dot = functools.partial(jnp.dot, preferred_element_type=jnp.float32)
+    return dot(ah, bh) + (dot(ah, bl) + dot(al, bh))
+
+
 def conv_kernel(
-    width, q_ref, k_ref, v_ref, taps_ref, toep_ref, leave_ref, reach_ref, fade_ref, skip_ref,
-    query_ref, base_ref, state_ref
+    width, q_ref, k_ref, v_ref, taps_ref, lags_ref, leave_ref, reach_ref, fade_ref, skip_ref,
+    query_ref, base_ref, state_ref, toep_ref
 ):
     taps = taps_ref.shape[0]
     count, lanes = query_ref.shape
@@ -56,7 +62,18 @@
     lane = lax.broadcasted_iota(jnp.int32, (SUB, lanes), 1) // width
     row = lax.broadcasted_iota(jnp.int32, (tile * order, lanes), 0) // order
     diagonal = row == lax.broadcasted_iota(jnp.int32, (tile * order, lanes), 1) // width
-    toep = toep_ref[...].reshape(tile * SUB, SUB)
+
+    @pl.when(pl.program_id(1) == 0)
+    def _():
+        below = lax.broadcasted_iota(jnp.int32, (SUB, SUB), 0) >= lax.broadcasted_iota(
+            jnp.int32, (SUB, SUB), 1
+        )
+        for g in range(tile):
+            wide = jnp.broadcast_to(lags_ref[g : g + 1], (SUB, SUB))
+            rolled = pltpu.roll(wide, 0, 1, stride=1, stride_axis=0)
+            toep_ref[g * SUB : (g + 1) * SUB] = jnp.where(below, rolled, 0.0).astype(jnp.bfloat16)
+
+    toep = toep_ref[...]
     state = jnp.zeros((tile * order, lanes), jnp.float32)
     for block in range(count // SUB):
         piece = gated[block * SUB : (block + 1) * SUB]
@@ -67,13 +84,9 @@
             picked = jnp.where(lane == g, wide[g * SUB : (g + 1) * SUB], picked)
         local = local + picked
         if block:
-            local = local + jnp.dot(
-                reach_ref[:SUB], state, precision=HIGHEST, preferred_element_type=jnp.float32
-            )
+            local = local + product3(reach_ref[:SUB], state)
         base_ref[block * SUB : (block + 1) * SUB] = local
-        fresh = jnp.dot(
-            leave_ref[...], piece, precision=HIGHEST, preferred_element_type=jnp.float32
-        )
+        fresh = product3(leave_ref[...], piece)
         state = fade_ref[...] * state + jnp.where(diagonal, fresh, 0.0)
     compact = state[:order]
     for g in range(1, tile):
@@ -81,7 +94,7 @@
     state_ref[...] = compact
 
 
-def convolved(proj, taps, toep, leave, reach, fade, skip, width, order, count):
+def convolved(proj, taps, lags, leave, reach, fade, skip, width, order, count):
     chans = skip.shape[1]
     lanes = min(LANES, chans)
     steps = chans // lanes
@@ -95,7 +108,7 @@
             pl.BlockSpec((None, rows, lanes), lambda i, j: (j, 0, steps + i)),
             pl.BlockSpec((None, rows, lanes), lambda i, j: (j, 0, 2 * steps + i)),
             pl.BlockSpec((taps.shape[0], 3, lanes), lambda i, j: (0, 0, i)),
-            pl.BlockSpec((tile, SUB, SUB), lambda i, j: (i, 0, 0)),
+            pl.BlockSpec((tile, SUB), lambda i, j: (i, 0)),
             pl.BlockSpec((tile * order, SUB), lambda i, j: (i, 0)),
             pl.BlockSpec((count, tile * order), lambda i, j: (0, i)),
             pl.BlockSpec((tile * order, 1), lambda i, j: (i, 0)),
@@ -111,11 +124,12 @@
             jax.ShapeDtypeStruct((segments, count, chans), jnp.float32),
             jax.ShapeDtypeStruct((segments, order, chans), jnp.float32),
         ],
+        scratch_shapes=[pltpu.VMEM((tile * SUB, SUB), jnp.bfloat16)],
         cost_estimate=pl.CostEstimate(
             flops=2 * count * chans * SUB * tile, bytes_accessed=count * chans * 20, transcendentals=0
         ),
         name="conv",
-    )(proj, proj, proj, taps, toep, leave, reach, fade, skip)
+    )(proj, proj, proj, taps, lags, leave, reach, fade, skip)
 
 
 def place():
@@ -146,102 +160,140 @@
 
 
 def gather_kernel(
-    own_ref, pieces_ref, tok_ref, w_ref, local_sems,
+    own_ref, pieces_ref, out_ref, tok_ref, w_ref, wo_ref, local_sems,
     line_send, line_recv, pass_send, pass_recv, pair_send, pair_recv,
     tp_send, tp_recv, core_send, core_recv, early_send, early_recv,
+    cols_send, cols_recv, swap_send, swap_recv,
 ):
     z, x, core, depth = place()
     parity = lax.rem(z, 2)
-    mate = z + 1 - 2 * parity
     n_tp, part = lax.axis_size("tp"), lax.axis_index("tp")
-    cols = own_ref.shape[1] // n_tp
     mine = index_of(z, x, core)
     side = {"seq": index_of(z, 1 - x, core)}
     twin = {"seq": index_of(z, x, 1 - core)}
-    pair = {"seq": index_of(mate, x, core)}
-
-    def on_line(step, other, sign):
-        there = lax.rem(z + sign * step + depth, depth)
-        return there, (1 - core if other else core)
+
+    def on_line(hop):
+        there = z ^ hop[0]
+        return there, (1 - core if hop[1] else core)
 
     hops = [(step, other) for step in range(depth) for other in range(2)][1:]
-    hops = sorted(hops, key=lambda hop: (min(hop[0], depth - hop[0]), hop))
-    peers = [side]
-    for hop in hops:
-        there, which = on_line(*hop, 1)
-        peers.append({"seq": index_of(there, x, which)})
+    peers = [side] + [
+        {"seq": index_of(there, x, which)} for there, which in map(on_line, hops)
+    ]
     tps = [{"tp": lax.rem(part + d, n_tp)} for d in range(1, n_tp)]
     greet(peers + tps)
 
-    def band(which):
-        return pl.ds(pl.multiple_of(which * cols, cols), cols)
+    cols = own_ref.shape[1] // (2 * n_tp)
+
+    def band(which, piece):
+        return pl.ds(pl.multiple_of((2 * which + piece) * cols, cols), cols)
 
     own_slot, mate_slot = 2 * parity + core, 2 * (1 - parity) + core
-    role = own_slot
     stay = [
         pltpu.make_async_copy(own_ref, tok_ref.at[own_slot], local_sems.at[0]),
-        pltpu.make_async_copy(pieces_ref.at[role], w_ref.at[mine], local_sems.at[1]),
+        pltpu.make_async_copy(pieces_ref.at[own_slot], w_ref.at[mine], local_sems.at[1]),
     ]
-    for copy in stay:
-        copy.start()
     started = []
 
-    def begin(copy):
+    def begin(*what):
+        copy = remote(*what)
         copy.start()
         started.append(copy)
         return copy
 
-    first = begin(remote(
-        pieces_ref.at[role], w_ref.at[mine], pass_send.at[0], pass_recv.at[0], side
-    ))
-    line = {}
-    paired = None
-    for n, hop in enumerate(hops):
-        if n == 4 or (n == len(hops) - 1 and paired is None):
-            paired = begin(remote(
-                own_ref.at[:, band(part)], tok_ref.at[own_slot, :, band(part)],
-                pair_send, pair_recv, pair,
-            ))
-        there, which = on_line(*hop, 1)
+    def to_line(hop):
+        there, which = on_line(hop)
         index = 2 * hop[0] + hop[1]
-        line[hop] = begin(remote(
+        return begin(
             pieces_ref.at[2 * lax.rem(there, 2) + which], w_ref.at[mine],
             line_send.at[index], line_recv.at[index], {"seq": index_of(there, x, which)},
-        ))
-    early = begin(remote(own_ref, tok_ref.at[own_slot], early_send, early_recv, twin))
+        )
+
+    def to_pair(piece):
+        where = tok_ref.at[own_slot, :, band(part, piece)]
+        return begin(
+            own_ref.at[:, band(part, piece)], where, pair_send.at[piece], pair_recv.at[piece],
+            {"seq": index_of(z ^ 1, x, core)},
+        )
+
+    quarter = wo_ref.shape[1] // 4
+    out_cols = wo_ref.shape[2]
+
+    def quarter_rows(piece):
+        return pl.ds(pl.multiple_of((2 * core + piece) * quarter, quarter), quarter)
+
+    def columns(d, piece):
+        target = lax.rem(part + d, n_tp)
+        slot = 2 * (d - 1) + piece
+        return begin(
+            out_ref.at[quarter_rows(piece), pl.ds(pl.multiple_of(target * out_cols, out_cols), out_cols)],
+            wo_ref.at[d - 1, quarter_rows(piece)],
+            cols_send.at[slot], cols_recv.at[slot], tps[d - 1],
+        )
+
+    def swap(d, piece):
+        slot = 2 * (d - 1) + piece
+        where = wo_ref.at[d - 1, quarter_rows(piece)]
+        return begin(where, where, swap_send.at[slot], swap_recv.at[slot], twin)
+
+    paired = [to_pair(0)]
+    first = begin(
+        pieces_ref.at[own_slot], w_ref.at[mine], pass_send.at[0], pass_recv.at[0], side
+    )
+    line = {}
+    for hop in hops[:2]:
+        line[hop] = to_line(hop)
+    paired.append(to_pair(1))
+    for hop in hops[2:]:
+        line[hop] = to_line(hop)
+    moved = {(d, 0): columns(d, 0) for d in range(1, n_tp)}
+    early = begin(own_ref, tok_ref.at[own_slot], early_send, early_recv, twin)
+    for copy in stay:
+        copy.start()
 
     forwards = []
 
     def hand_on(hop):
         index = 2 * hop[0] + hop[1]
-        there, which = on_line(*hop, -1)
-        source = index_of(there, x, which)
+        source = index_of(on_line(hop)[0], x, on_line(hop)[1])
         line[hop].wait_recv()
-        forwards.append(begin(remote(
+        forwards.append(begin(
             w_ref.at[source], w_ref.at[source], pass_send.at[index], pass_recv.at[index], side
-        )))
-
-    def to_twin(which, slot):
-        return begin(remote(
-            tok_ref.at[mate_slot, :, band(which)], tok_ref.at[mate_slot, :, band(which)],
-            core_send.at[slot], core_recv.at[slot], twin,
         ))
 
-    for hop in hops[:4]:
-        hand_on(hop)
-    paired.wait_recv()
-    across = []
+    twins, across = [], {}
+
+    def to_twin(which, piece, d):
+        where = tok_ref.at[mate_slot, :, band(which, piece)]
+        slot = 2 * d + piece
+        twins.append(begin(where, where, core_send.at[slot], core_recv.at[slot], twin))
+
+    def pair_on(piece):
+        paired[piece].wait_recv()
+        where = tok_ref.at[mate_slot, :, band(part, piece)]
+        for d in range(1, n_tp):
+            slot = 2 * (d - 1) + piece
+            across[d, piece] = begin(
+                where, where, tp_send.at[slot], tp_recv.at[slot], tps[d - 1]
+            )
+        to_twin(part, piece, 0)
+
+    hand_on(hops[0])
+    pair_on(0)
+    hand_on(hops[1])
+    hand_on(hops[3])
+    pair_on(1)
     for d in range(1, n_tp):
-        across.append(begin(remote(
-            tok_ref.at[mate_slot, :, band(part)], tok_ref.at[mate_slot, :, band(part)],
-            tp_send.at[d - 1], tp_recv.at[d - 1], tps[d - 1],
-        )))
-    twins = [to_twin(part, 0)]
+        moved[d, 1] = columns(d, 1)
+    hand_on(hops[2])
     for hop in hops[4:]:
         hand_on(hop)
-    for d in range(1, n_tp):
-        across[d - 1].wait_recv()
-        twins.append(to_twin(lax.rem(part - d + n_tp, n_tp), d))
+    for piece in range(2):
+        for d in range(1, n_tp):
+            moved[d, piece].wait_recv()
+            twins.append(swap(d, piece))
+            across[d, piece].wait_recv()
+            to_twin(lax.rem(part - d + n_tp, n_tp), piece, d)
     for copy in [first, early] + forwards + twins:
         copy.wait_recv()
     for copy in started:
@@ -250,37 +302,26 @@
         copy.wait()
 
 
-def gathered(own, pieces):
+def gathered(own, pieces, w_out):
     size, n_tp = lax.axis_size("seq"), lax.axis_size("tp")
     line = size // 2
     anywhere = pl.BlockSpec(memory_space=pl.ANY)
-    one = pltpu.SemaphoreType.DMA(())
+    counts = [2, line, line, line, line, 2, 2] + [2 * n_tp] * 4 + [0, 0] + [2 * n_tp] * 4
     return pl.pallas_call(
         gather_kernel,
         out_shape=[
             jax.ShapeDtypeStruct((4,) + own.shape, own.dtype),
             jax.ShapeDtypeStruct((size,) + pieces.shape[1:], pieces.dtype),
-        ],
-        in_specs=[anywhere, anywhere],
-        out_specs=[anywhere, anywhere],
-        scratch_shapes=[
-            pltpu.SemaphoreType.DMA((2,)),
-            pltpu.SemaphoreType.DMA((line,)),
-            pltpu.SemaphoreType.DMA((line,)),
-            pltpu.SemaphoreType.DMA((line,)),
-            pltpu.SemaphoreType.DMA((line,)),
-            one,
-            one,
-            pltpu.SemaphoreType.DMA((n_tp,)),
-            pltpu.SemaphoreType.DMA((n_tp,)),
-            pltpu.SemaphoreType.DMA((n_tp,)),
-            pltpu.SemaphoreType.DMA((n_tp,)),
-            one,
-            one,
-        ],
+            jax.ShapeDtypeStruct(
+                (n_tp - 1, w_out.shape[0], w_out.shape[1] // n_tp), w_out.dtype
+            ),
+        ],
+        in_specs=[anywhere] * 3,
+        out_specs=[anywhere] * 3,
+        scratch_shapes=[pltpu.SemaphoreType.DMA((n,) if n else ()) for n in counts],
         compiler_params=pltpu.CompilerParams(collective_id=0, has_side_effects=True),
         name="gather",
-    )(own, pieces)
+    )(own, pieces, w_out)
 
 
 def share_kernel(own_ref, all_ref, send_sems, recv_sems):
@@ -322,42 +363,68 @@
     )(state)
 
 
-def spread_kernel(mix_ref, full_ref, local_sem, send_sems, recv_sems):
+def spread_kernel(mix_ref, full_ref, local_sem, send_sems, recv_sems, tp_send, tp_recv):
     z, x, core, _ = place()
+    chans = mix_ref.shape[2]
+    n_tp, part = lax.axis_size("tp"), lax.axis_index("tp")
     parity = lax.rem(z, 2)
     me = 2 * parity + core
-    base = 2 * (z // 2)
 
     def peer(d):
-        there = lax.rem(me + d, 4)
-        return there, {"seq": index_of(base + there // 2, x, lax.rem(there, 2))}
-
-    greet([peer(d)[1] for d in range(1, 4)])
+        there = (z ^ (d // 2), (1 - core if d % 2 else core))
+        return 2 * lax.rem(there[0], 2) + there[1], {"seq": index_of(there[0], x, there[1])}
+
+    tps = [{"tp": lax.rem(part + d, n_tp)} for d in range(1, n_tp)]
+    greet([peer(d)[1] for d in range(1, 4)] + tps)
+
+    def at(slot, which):
+        return full_ref.at[slot, :, pl.ds(pl.multiple_of(which * chans, chans), chans)]
+
+    across = []
+
+    def over(source, which, n):
+        for d in range(1, n_tp):
+            sem = 4 * (d - 1) + n
+            copy = remote(source, at(d, which), tp_send.at[sem], tp_recv.at[sem], tps[d - 1])
+            copy.start()
+            across.append(copy)
+
     copies = []
-    for d in (2, 1, 3):
+    for d in (2, 3, 1):
         there, device = peer(d)
         copy = remote(
-            mix_ref.at[there], full_ref.at[me], send_sems.at[d - 1], recv_sems.at[d - 1], device
+            mix_ref.at[there], at(0, me), send_sems.at[d - 1], recv_sems.at[d - 1], device
         )
         copy.start()
-        copies.append(copy)
-    stay = pltpu.make_async_copy(mix_ref.at[me], full_ref.at[me], local_sem)
+        copies.append((d, copy))
+    over(mix_ref.at[me], me, 0)
+    stay = pltpu.make_async_copy(mix_ref.at[me], at(0, me), local_sem)
     stay.start()
-    for copy in copies:
+    for d, copy in copies[2:] + copies[:2]:
+        copy.wait_recv()
+        which = peer(d)[0]
+        over(at(0, which), which, d)
+    for _, copy in copies:
+        copy.wait_send()
+    for copy in across:
         copy.wait()
     stay.wait()
 
 
 def spread(mix):
+    n_tp = lax.axis_size("tp")
+    roles, count, chans = mix.shape
     return pl.pallas_call(
         spread_kernel,
-        out_shape=jax.ShapeDtypeStruct(mix.shape, mix.dtype),
+        out_shape=jax.ShapeDtypeStruct((n_tp, count, roles * chans), mix.dtype),
         in_specs=[pl.BlockSpec(memory_space=pltpu.VMEM)],
         out_specs=pl.BlockSpec(memory_space=pltpu.VMEM),
         scratch_shapes=[
             pltpu.SemaphoreType.DMA(()),
             pltpu.SemaphoreType.DMA((3,)),
             pltpu.SemaphoreType.DMA((3,)),
+            pltpu.SemaphoreType.DMA((4 * n_tp,)),
+            pltpu.SemaphoreType.DMA((4 * n_tp,)),
         ],
         compiler_params=pltpu.CompilerParams(collective_id=2, has_side_effects=True),
         name="spread",
@@ -367,12 +434,7 @@
 def mix_kernel(width, query_ref, base_ref, all_ref, weight_ref, reach_ref, mix_ref):
     order = all_ref.shape[1]
     entering = jnp.sum(all_ref[...] * weight_ref[...], axis=0)
-    carried = jnp.dot(
-        reach_ref[...],
-        fanned(entering, width, order),
-        precision=HIGHEST,
-        preferred_element_type=jnp.float32,
-    )
+    carried = product3(reach_ref[...], fanned(entering, width, order))
     mix_ref[...] = (query_ref[...] * (base_ref[...] + carried)).astype(mix_ref.dtype)
 
 
@@ -413,7 +475,7 @@
         [jnp.zeros((HALO - (taps - 1), tokens.shape[1]), tokens.dtype), before, tokens], axis=0
     )
     pieces = w_in.reshape(rows, 3, 4, chans).transpose(2, 0, 1, 3).reshape(4, rows, 3 * chans)
-    tok, weights = gathered(extended, pieces)
+    tok, weights, out_rows = gathered(extended, pieces, w_out)
 
     def own(array, axis):
         share = array.shape[axis] // 4
@@ -424,14 +486,13 @@
     groups, order = decay_rate.shape
     weight_mode = residue * jnp.sqrt(2.0 * decay_rate / order)
     offsets = jnp.arange(SUB, dtype=jnp.float32)
-    kernel = jnp.einsum(
+    back = (-jnp.arange(SUB) % SUB).astype(jnp.float32)
+    lags = jnp.einsum(
         "gm,gmd->gd",
         weight_mode,
-        jnp.exp(-decay_rate[:, :, None] * offsets[None, None, :]),
+        jnp.exp(-decay_rate[:, :, None] * back[None, None, :]),
         precision=HIGHEST,
     )
-    lag = jnp.arange(SUB)[:, None] - jnp.arange(SUB)[None, :]
-    toep = jnp.where(lag[None] >= 0, kernel[:, jnp.maximum(lag, 0)], 0.0).astype(jnp.bfloat16)
     rate = decay_rate.reshape(groups * order)
     leave = jnp.exp(-rate[:, None] * (SUB - 1.0 - offsets[None, :]))
     fade = jnp.exp(-rate * SUB)[:, None]
@@ -455,30 +516,17 @@
         preferred_element_type=jnp.float32,
     ).astype(jnp.bfloat16).reshape(4, -1, 3 * chans)
     query, base, final = convolved(
-        proj, short_taps, toep, leave, reach, fade, skip, width, order, count
+        proj, short_taps, lags, leave, reach, fade, skip, width, order, count
     )
     everything = shared(final).reshape(-1, order, chans)
-    mix = spread(mixed_of(query, base, everything, weight, reach, width))
-    full = mix.transpose(1, 0, 2).reshape(count, 4 * chans)
+    full = spread(mixed_of(query, base, everything, weight, reach, width))
 
     share = w_out.shape[1] // n_tp
-    half = share // 2
-
-    def product(target, piece):
-        cols = lax.dynamic_slice_in_dim(w_out, target * share + piece * half, half, axis=1)
-        return jnp.dot(full, cols, preferred_element_type=jnp.float32).astype(jnp.bfloat16)
-
-    arrived = []
+    kept = lax.dynamic_slice_in_dim(w_out, part * share, share, axis=1)
+    total = jnp.dot(full[0], kept, preferred_element_type=jnp.float32)
     for d in range(1, n_tp):
-        for piece in range(2):
-            arrived.append(rotated(product((part + d) % n_tp, piece), "tp", d))
-    results = []
-    for piece in range(2):
-        total = product(part, piece).astype(jnp.float32)
-        for d in range(1, n_tp):
-            total = total + arrived[2 * (d - 1) + piece].astype(jnp.float32)
-        results.append(total.astype(jnp.bfloat16))
-    return jnp.concatenate(results, axis=1)
+        total = total + jnp.dot(full[d], out_rows[d - 1], preferred_element_type=jnp.float32)
+    return total.astype(jnp.bfloat16)
 
 
 def solution(mesh):

time: 477 us -> 382 us (0.80)
  local copies, waits for them, and re-layouts: 76.9 us -> 14.8 us
  waiting for transfers between devices: 35.7 us -> 0.01 us
    gather x2 -> x0, local copies, waits for them, and re-layouts: 61.8 us -> none  [shards(): kernel[:, jnp.maximum(lag, 0)]]
    ppermute x2 -> x0, waiting for transfers between devices: 35.6 us -> none  [rotated(): lax.ppermute(block, axis, [(i, (i + distance) % size) for i in range(size)])]
    pallas_call x1, Pallas kernels: 27.9 us -> 52.1 us  [spread(): pl.pallas_call(spread_kernel, out_shape=jax.ShapeDtypeStruct((n_tp, count...]
    pallas_call x1, Pallas kernels: 208 us -> 191 us  [gathered(): pl.pallas_call(gather_kernel, out_shape=[jax.ShapeDtypeStruct((4,) + own....]
    pallas_call x1, Pallas kernels: 30.1 us -> 25.3 us  [convolved(): pl.pallas_call(functools.partial(conv_kernel, width), grid=(steps, segmen...]
    dot_general x4 -> x3, matrix products: 19.8 us -> 19.6 us  [the longest x1 9.2 us: shards(): jnp.dot(full[d], out_rows[d - 1], preferred_element_type=jnp.float32)]
  transfers between devices with their start and end apart: 3 -> 1, of which waited for: 2 -> 0; matrix products, arithmetic and copies ran while one was open for 19% -> 7% of each run, Pallas kernels for 0% -> 0%
where the time goes in v3:
time: 382 us; the launch traced here: 381 us
  Pallas kernels  293 us (77%)
  matrix products  54.1 us (14%)
  other arithmetic  16.7 us (4%)
  local copies, waits for them, and re-layouts  14.8 us (4%)
    pallas_call x1, Pallas kernels, gathered(): pl.pallas_call(gather_kernel, out_shape=[jax.ShapeDtypeStruct((4,) + own....  191 us
    pallas_call x1, Pallas kernels, spread(): pl.pallas_call(spread_kernel, out_shape=jax.ShapeDtypeStruct((n_tp, count...  52.1 us
    dot_general x1, matrix products, shards(): jnp.dot(tok.reshape(-1, tok.shape[2]), weights.reshape(-1, weights.shape[...  34.5 us
    pallas_call x1, Pallas kernels, convolved(): pl.pallas_call(functools.partial(conv_kernel, width), grid=(steps, segmen...  25.3 us
    pallas_call x1, Pallas kernels, shared(): pl.pallas_call(share_kernel, out_shape=jax.ShapeDtypeStruct((total,) + st...  15.3 us
    pallas_call x1, Pallas kernels, mixed_of(): pl.pallas_call(functools.partial(mix_kernel, width), grid=(chans // lanes...  9.26 us
    dot_general x1, matrix products, shards(): jnp.dot(full[d], out_rows[d - 1], preferred_element_type=jnp.float32)  9.2 us
    dot_general x1, matrix products, shards(): total = jnp.dot(full[0], kept, preferred_element_type=jnp.float32)  8.6 us
  transfers between devices with their start and end apart: 1, of which 0 were waited for; matrix products, arithmetic and copies ran while one was open for 7% of the time, Pallas kernels for 0%

profile of v3, /device:TPU:0, one launch (start us, length us, event | category | flops | bytes accessed | tf_op | source)
XLA Modules:
  0.0 381.3 jit_solution(3004203724350190023)
XLA Ops:
  0.0 1.6 slice.9
  1.6 3.0 collective-permute-start
  7.1 0.7 subtract_compare_fusion
  7.7 1.4 multiply_exponential_fusion.1
  9.2 0.7 copy.25
  10.6 0.7 mul.153
  11.6 1.8 fusion.10
  13.3 1.5 multiply_exponential_fusion.leave_ref
  14.8 1.9 exponential_multiply_fusion.reach_ref
  16.7 2.4 exponential_select_fusion.weight_ref
  19.7 2.8 copy.17
  22.5 2.1 copy.18
  24.7 2.8 copy.19.pieces_ref
  27.6 0.9 exp.31.fade_ref
  28.4 1.3 dynamic-slice.3
  29.8 6.4 %pad_maximum_fusion.own_ref = bf16[528,4096]{1,0:T(8,128)(2,1)} fusion(bf16[512,4096]{1,0:T(8,128)(2,1)} %param.7, bf16[2,4096]{1,0:T(2,128)(2,1)} %collective-permute-done, bf16[528]{0:T(1024)(128)(2,1)S(1)} %pad.clone), kind=kLoop, calls=%fused_computation.5 | loop fusion | flops 12976128 | bytes 8537120 | tf_op jit(solution)/shard_map/concatenate | solution.py:474
  36.2 190.8 %gather.1 = (bf16[4,528,4096]{2,1,0:T(8,128)(2,1)}, bf16[16,256,1536]{2,1,0:T(8,128)(2,1)}, bf16[1,2048,2048]{2,1,0:T(8,128)(2,1)}) custom-call(bf16[528,4096]{1,0:T(8,128)(2,1)} %pad_maximum_fusion.own_ref, bf16[4,256,1536]{2,1,0:T(8,128)(2,1)} %copy.19.pieces_ref, bf16[2048,4096]{1,0:T(8,128)(2,1)} %out_ref.1), custom_call_target="tpu_custom_call" | custom-call | tf_op jit(solution)/shard_map/gather/pallas_call | solution.py:310
  227.0 34.5 %convolution_convert_fusion = bf16[2112,1536]{1,0:T(8,128)(2,1)} fusion(bf16[2112,4096]{1,0:T(8,128)(2,1)} %bitcast.37, bf16[4096,1536]{1,0:T(8,128)(2,1)} %bitcast.38), kind=kOutput, calls=%fused_computation | convolution fusion | flops 26578354176 | bytes 36372480 | tf_op jit(solution)/shard_map/dot_general | solution.py:513
  261.5 25.3 %conv.1 = (f32[4,512,512]{2,1,0:T(8,128)}, f32[4,512,512]{2,1,0:T(8,128)}, f32[4,16,512]{2,1,0:T(8,128)}) custom-call(bf16[4,528,1536]{2,1,0:T(8,128)(2,1)} %bitcast.27, bf16[4,528,1536]{2,1,0:T(8,128)(2,1)} %bitcast.28, bf16[4,528,1536]{2,1,0:T(8,128)(2,1)} %bitcast.29, f32[3,3,512]{2,1,0:T(4,128)} %constant_dynamic-slice_fusion.taps_ref, ...), custom_call_target="tpu_custom_call" | custom-call | flops 1073741824 | bytes 5242880 | tf_op jit(solution)/shard_map/conv/pallas_call | solution.py:103
  286.8 15.3 %share.1 = f32[4,4,16,512]{3,2,1,0:T(8,128)} custom-call(f32[4,16,512]{2,1,0:T(8,128)} %get-tuple-element.15.own_ref), custom_call_target="tpu_custom_call" | custom-call | tf_op jit(solution)/shard_map/share/pallas_call | solution.py:352
  302.1 9.3 %mix.1.mix_ref = bf16[4,512,512]{2,1,0:T(8,128)(2,1)} custom-call(f32[4,512,512]{2,1,0:T(8,128)} %get-tuple-element.13.query_ref, f32[4,512,512]{2,1,0:T(8,128)} %get-tuple-element.14.base_ref, f32[16,16,512]{2,1,0:T(8,128)} %bitcast.32, f32[4,16,16,512]{3,2,1,0:T(8,128)} %exponential_select_fusion.weight_ref, f32[512,512]{1,0:T(8,128)} %exponential_multiply_fusion.reach_ref), custom_call_target="tpu_custom_call" | custom-call | tf_op jit(solution)/shard_map/mix/pallas_call | solution.py:446
  311.4 52.1 %spread.1 = bf16[2,512,2048]{2,1,0:T(8,128)(2,1)} custom-call(bf16[4,512,512]{2,1,0:T(8,128)(2,1)} %mix.1.mix_ref), custom_call_target="tpu_custom_call" | custom-call | tf_op jit(solution)/shard_map/spread/pallas_call | solution.py:417
  363.5 8.6 %fusion.2 = f32[512,2048]{1,0:T(8,128)S(1)} fusion(bf16[2048,4096]{1,0:T(8,128)(2,1)} %out_ref.1, s32[]{:T(128)S(6)} %select_n.100, bf16[2,512,2048]{2,1,0:T(8,128)(2,1)} %spread.1), kind=kOutput, calls=%fused_computation.3 | convolution fusion | flops 4294967296 | bytes 14680068 | tf_op jit(solution)/shard_map/dot_general | solution.py:526
  372.1 9.2 %add_convert_fusion = bf16[512,2048]{1,0:T(8,128)(2,1)} fusion(f32[512,2048]{1,0:T(8,128)S(1)} %fusion.2, bf16[1,2048,2048]{2,1,0:T(8,128)(2,1)} %get-tuple-element.16, bf16[2,512,2048]{2,1,0:T(8,128)(2,1)S(1)} %copy-done.2), kind=kOutput, calls=%fused_computation.6 | convolution fusion | flops 4297064448 | bytes 16777216 | tf_op jit(solution)/shard_map/dot_general | solution.py:528
  (29 shorter events, 4.3 us)
Async XLA Ops:
  0.0 19.1 %copy-start = (f32[3,3,2048]{2,1,0:T(4,128)S(1)}, f32[3,3,2048]{2,1,0:T(4,128)}, u32[]{:S(2)}) copy-start(f32[3,3,2048]{2,1,0:T(4,128)} %param.9) | copy-start | bytes 221188
  0.0 19.7 %copy-start.3 = (bf16[256,3,2048]{2,0,1:T(8,128)(2,1)S(1)}, bf16[256,3,2048]{2,0,1:T(8,128)(2,1)}, u32[]{:S(2)}) copy-start(bf16[256,3,2048]{2,0,1:T(8,128)(2,1)} %param.8) | copy-start | bytes 9437188
  1.6 28.2 %collective-permute-start = (bf16[2,4096]{1,0:T(2,128)(2,1)}, bf16[2,4096]{1,0:T(2,128)(2,1)}, u32[]{:S(2)}, u32[]{:S(2)}) collective-permute-start(bf16[2,4096]{1,0:T(2,128)(2,1)} %slice.9), channel_id=1, source_target_pairs={{0,2},{2,4},{4,6},{6,8},{8,10},{10,12},{12,14},{14,16},{16,18},{18... | collective-permute-start | bytes 49160 | tf_op jit(solution)/shard_map/ppermute | solution.py:20
  24.6 2.9 copy-start.4
  363.5 8.6 %copy-start.2 = (bf16[2,512,2048]{2,1,0:T(8,128)(2,1)S(1)}, bf16[2,512,2048]{2,1,0:T(8,128)(2,1)}, u32[]{:S(2)}) copy-start(bf16[2,512,2048]{2,1,0:T(8,128)(2,1)} %spread.1) | copy-start | bytes 12582916
  372.1 9.2 %copy-start.1 = (f32[3,3,2048]{2,1,0:T(4,128)S(1)}, f32[3,3,2048]{2,1,0:T(4,128)}, u32[]{:S(2)}) copy-start(f32[3,3,2048]{2,1,0:T(4,128)} %param.9) | copy-start | bytes 221188

commit v4 on v3

--- a/solution.py
+++ b/solution.py
@@ -160,10 +160,10 @@
 
 
 def gather_kernel(
-    own_ref, pieces_ref, out_ref, tok_ref, w_ref, wo_ref, local_sems,
+    own_ref, halo_ref, pieces_ref, out_ref, tok_ref, w_ref, wo_ref, held_ref, held_w_ref, local_sems,
     line_send, line_recv, pass_send, pass_recv, pair_send, pair_recv,
     tp_send, tp_recv, core_send, core_recv, early_send, early_recv,
-    cols_send, cols_recv, swap_send, swap_recv,
+    cols_send, cols_recv, swap_send, swap_recv, halo_send, halo_recv,
 ):
     z, x, core, depth = place()
     parity = lax.rem(z, 2)
@@ -189,10 +189,19 @@
         return pl.ds(pl.multiple_of((2 * which + piece) * cols, cols), cols)
 
     own_slot, mate_slot = 2 * parity + core, 2 * (1 - parity) + core
+    body = pl.ds(HALO, own_ref.shape[0])
+    head = pl.ds(0, HALO)
+    taken = [
+        pltpu.make_async_copy(own_ref, held_ref.at[body], local_sems.at[0]),
+        pltpu.make_async_copy(halo_ref, held_ref.at[head], local_sems.at[1]),
+        pltpu.make_async_copy(pieces_ref.at[own_slot], held_w_ref, local_sems.at[2]),
+    ]
     stay = [
-        pltpu.make_async_copy(own_ref, tok_ref.at[own_slot], local_sems.at[0]),
-        pltpu.make_async_copy(pieces_ref.at[own_slot], w_ref.at[mine], local_sems.at[1]),
+        pltpu.make_async_copy(held_ref, tok_ref.at[own_slot], local_sems.at[3]),
+        pltpu.make_async_copy(held_w_ref, w_ref.at[mine], local_sems.at[4]),
     ]
+    for copy in taken:
+        copy.start()
     started = []
 
     def begin(*what):
@@ -210,7 +219,7 @@
         )
 
     def to_pair(piece):
-        where = tok_ref.at[own_slot, :, band(part, piece)]
+        where = tok_ref.at[own_slot, body, band(part, piece)]
         return begin(
             own_ref.at[:, band(part, piece)], where, pair_send.at[piece], pair_recv.at[piece],
             {"seq": index_of(z ^ 1, x, core)},
@@ -247,7 +256,16 @@
     for hop in hops[2:]:
         line[hop] = to_line(hop)
     moved = {(d, 0): columns(d, 0) for d in range(1, n_tp)}
-    early = begin(own_ref, tok_ref.at[own_slot], early_send, early_recv, twin)
+    early = begin(own_ref, tok_ref.at[own_slot, body], early_send, early_recv, twin)
+    heads = []
+    for n, hop in enumerate(hops[:3]):
+        there, which = on_line(hop)
+        heads.append(begin(
+            halo_ref, tok_ref.at[own_slot, head], halo_send.at[n], halo_recv.at[n],
+            {"seq": index_of(there, x, which)},
+        ))
+    for copy in taken:
+        copy.wait()
     for copy in stay:
         copy.start()
 
@@ -264,13 +282,13 @@
     twins, across = [], {}
 
     def to_twin(which, piece, d):
-        where = tok_ref.at[mate_slot, :, band(which, piece)]
+        where = tok_ref.at[mate_slot, body, band(which, piece)]
         slot = 2 * d + piece
         twins.append(begin(where, where, core_send.at[slot], core_recv.at[slot], twin))
 
     def pair_on(piece):
         paired[piece].wait_recv()
-        where = tok_ref.at[mate_slot, :, band(part, piece)]
+        where = tok_ref.at[mate_slot, body, band(part, piece)]
         for d in range(1, n_tp):
             slot = 2 * (d - 1) + piece
             across[d, piece] = begin(
@@ -294,7 +312,7 @@
             twins.append(swap(d, piece))
             across[d, piece].wait_recv()
             to_twin(lax.rem(part - d + n_tp, n_tp), piece, d)
-    for copy in [first, early] + forwards + twins:
+    for copy in [first, early] + heads + forwards + twins:
         copy.wait_recv()
     for copy in started:
         copy.wait_send()
@@ -302,26 +320,30 @@
         copy.wait()
 
 
-def gathered(own, pieces, w_out):
+def gathered(own, halo, pieces, w_out):
     size, n_tp = lax.axis_size("seq"), lax.axis_size("tp")
     line = size // 2
     anywhere = pl.BlockSpec(memory_space=pl.ANY)
-    counts = [2, line, line, line, line, 2, 2] + [2 * n_tp] * 4 + [0, 0] + [2 * n_tp] * 4
+    counts = [5, line, line, line, line, 2, 2] + [2 * n_tp] * 4 + [0, 0] + [2 * n_tp] * 4 + [3, 3]
     return pl.pallas_call(
         gather_kernel,
         out_shape=[
-            jax.ShapeDtypeStruct((4,) + own.shape, own.dtype),
+            jax.ShapeDtypeStruct((4, HALO + own.shape[0], own.shape[1]), own.dtype),
             jax.ShapeDtypeStruct((size,) + pieces.shape[1:], pieces.dtype),
             jax.ShapeDtypeStruct(
                 (n_tp - 1, w_out.shape[0], w_out.shape[1] // n_tp), w_out.dtype
             ),
         ],
-        in_specs=[anywhere] * 3,
+        in_specs=[anywhere] * 4,
         out_specs=[anywhere] * 3,
-        scratch_shapes=[pltpu.SemaphoreType.DMA((n,) if n else ()) for n in counts],
+        scratch_shapes=[
+            pltpu.VMEM((HALO + own.shape[0], own.shape[1]), own.dtype),
+            pltpu.VMEM(pieces.shape[1:], pieces.dtype),
+        ]
+        + [pltpu.SemaphoreType.DMA((n,) if n else ()) for n in counts],
         compiler_params=pltpu.CompilerParams(collective_id=0, has_side_effects=True),
         name="gather",
-    )(own, pieces, w_out)
+    )(own, halo, pieces, w_out)
 
 
 def share_kernel(own_ref, all_ref, send_sems, recv_sems):
@@ -471,11 +493,9 @@
     chans = all_chans // 4
 
     before = shifted_by(tokens[count - (taps - 1) :], "seq", 1)
-    extended = jnp.concatenate(
-        [jnp.zeros((HALO - (taps - 1), tokens.shape[1]), tokens.dtype), before, tokens], axis=0
-    )
+    halo = jnp.pad(before, ((HALO - (taps - 1), 0), (0, 0)))
     pieces = w_in.reshape(rows, 3, 4, chans).transpose(2, 0, 1, 3).reshape(4, rows, 3 * chans)
-    tok, weights, out_rows = gathered(extended, pieces, w_out)
+    tok, weights, out_rows = gathered(tokens, halo, pieces, w_out)
 
     def own(array, axis):
         share = array.shape[axis] // 4

time: 382 us -> 375 us (0.982)
  other arithmetic: 16.7 us -> 10.3 us
    concatenate x1 -> x0, other arithmetic: 6.44 us -> none  [shards(): jnp.concatenate([jnp.zeros((HALO - (taps - 1), tokens.shape[1]), tokens.d...]
where the time goes in v4:
time: 375 us; the launch traced here: 373 us
  Pallas kernels  291 us (78%)
  matrix products  53.2 us (14%)
  local copies, waits for them, and re-layouts  16.2 us (4%)
  other arithmetic  10.3 us (3%)
    pallas_call x1, Pallas kernels, gathered(): pl.pallas_call(gather_kernel, out_shape=[jax.ShapeDtypeStruct((4, HALO +...  189 us
    pallas_call x1, Pallas kernels, spread(): pl.pallas_call(spread_kernel, out_shape=jax.ShapeDtypeStruct((n_tp, count...  51.3 us
    dot_general x1, matrix products, shards(): jnp.dot(tok.reshape(-1, tok.shape[2]), weights.reshape(-1, weights.shape[...  34.5 us
    pallas_call x1, Pallas kernels, convolved(): pl.pallas_call(functools.partial(conv_kernel, width), grid=(steps, segmen...  25.3 us
    pallas_call x1, Pallas kernels, shared(): pl.pallas_call(share_kernel, out_shape=jax.ShapeDtypeStruct((total,) + st...  16 us
    pallas_call x1, Pallas kernels, mixed_of(): pl.pallas_call(functools.partial(mix_kernel, width), grid=(chans // lanes...  9.22 us
    dot_general x1, matrix products, shards(): jnp.dot(full[d], out_rows[d - 1], preferred_element_type=jnp.float32)  9.2 us
    dot_general x1, matrix products, shards(): total = jnp.dot(full[0], kept, preferred_element_type=jnp.float32)  7.73 us
  transfers between devices with their start and end apart: 1, of which 0 were waited for; matrix products, arithmetic and copies ran while one was open for 7% of the time, Pallas kernels for 0%

profile of v4, /device:TPU:0, one launch (start us, length us, event | category | flops | bytes accessed | tf_op | source)
XLA Modules:
  0.0 373.3 jit_solution(15840179019738800598)
XLA Ops:
  0.0 1.6 slice.9
  1.6 3.0 collective-permute-start
  6.5 0.7 fusion.16
  7.8 1.4 multiply_exponential_fusion.1
  9.3 0.7 copy.25
  10.0 0.7 neg.48
  11.6 1.8 fusion.10
  13.4 1.5 multiply_exponential_fusion.leave_ref
  14.9 1.9 exponential_multiply_fusion.reach_ref
  16.8 2.4 exponential_select_fusion.weight_ref
  19.8 2.8 copy.17
  22.6 2.1 copy.18
  24.7 2.8 copy.19.pieces_ref
  27.6 0.9 exp.31.fade_ref
  28.5 1.3 dynamic-slice.3
  29.8 1.4 pad.4.halo_ref
  31.2 188.8 %gather.1 = (bf16[4,528,4096]{2,1,0:T(8,128)(2,1)}, bf16[16,256,1536]{2,1,0:T(8,128)(2,1)}, bf16[1,2048,2048]{2,1,0:T(8,128)(2,1)}) custom-call(bf16[512,4096]{1,0:T(8,128)(2,1)} %own_ref.1, bf16[16,4096]{1,0:T(8,128)(2,1)} %pad.4.halo_ref, bf16[4,256,1536]{2,1,0:T(8,128)(2,1)} %copy.19.pieces_ref, bf16[2048,4096]{1,0:T(8,128)(2,1)} %out_ref.1), custom_call_target="tpu_custom_call" | custom-call | tf_op jit(solution)/shard_map/gather/pallas_call | solution.py:328
  220.0 34.5 %convolution_convert_fusion = bf16[2112,1536]{1,0:T(8,128)(2,1)} fusion(bf16[2112,4096]{1,0:T(8,128)(2,1)} %bitcast.37, bf16[4096,1536]{1,0:T(8,128)(2,1)} %bitcast.38), kind=kOutput, calls=%fused_computation | convolution fusion | flops 26578354176 | bytes 36372480 | tf_op jit(solution)/shard_map/dot_general | solution.py:533
  254.5 25.3 %conv.1 = (f32[4,512,512]{2,1,0:T(8,128)}, f32[4,512,512]{2,1,0:T(8,128)}, f32[4,16,512]{2,1,0:T(8,128)}) custom-call(bf16[4,528,1536]{2,1,0:T(8,128)(2,1)} %bitcast.27, bf16[4,528,1536]{2,1,0:T(8,128)(2,1)} %bitcast.28, bf16[4,528,1536]{2,1,0:T(8,128)(2,1)} %bitcast.29, f32[3,3,512]{2,1,0:T(4,128)} %constant_dynamic-slice_fusion.taps_ref, ...), custom_call_target="tpu_custom_call" | custom-call | flops 1073741824 | bytes 5242880 | tf_op jit(solution)/shard_map/conv/pallas_call | solution.py:103
  279.8 16.0 %share.1 = f32[4,4,16,512]{3,2,1,0:T(8,128)} custom-call(f32[4,16,512]{2,1,0:T(8,128)} %get-tuple-element.15.own_ref), custom_call_target="tpu_custom_call" | custom-call | tf_op jit(solution)/shard_map/share/pallas_call | solution.py:374
  295.8 9.2 %mix.1.mix_ref = bf16[4,512,512]{2,1,0:T(8,128)(2,1)} custom-call(f32[4,512,512]{2,1,0:T(8,128)} %get-tuple-element.13.query_ref, f32[4,512,512]{2,1,0:T(8,128)} %get-tuple-element.14.base_ref, f32[16,16,512]{2,1,0:T(8,128)} %bitcast.32, f32[4,16,16,512]{3,2,1,0:T(8,128)} %exponential_select_fusion.weight_ref, f32[512,512]{1,0:T(8,128)} %exponential_multiply_fusion.reach_ref), custom_call_target="tpu_custom_call" | custom-call | tf_op jit(solution)/shard_map/mix/pallas_call | solution.py:468
  305.1 51.3 %spread.1 = bf16[2,512,2048]{2,1,0:T(8,128)(2,1)} custom-call(bf16[4,512,512]{2,1,0:T(8,128)(2,1)} %mix.1.mix_ref), custom_call_target="tpu_custom_call" | custom-call | tf_op jit(solution)/shard_map/spread/pallas_call | solution.py:439
  356.4 7.7 %fusion.2 = f32[512,2048]{1,0:T(8,128)S(1)} fusion(bf16[2048,4096]{1,0:T(8,128)(2,1)} %out_ref.1, s32[]{:T(128)S(6)} %select_n.100, bf16[2,512,2048]{2,1,0:T(8,128)(2,1)} %spread.1), kind=kOutput, calls=%fused_computation.3 | convolution fusion | flops 4294967296 | bytes 14680068 | tf_op jit(solution)/shard_map/dot_general | solution.py:546
  364.1 9.2 %add_convert_fusion = bf16[512,2048]{1,0:T(8,128)(2,1)} fusion(f32[512,2048]{1,0:T(8,128)S(1)} %fusion.2, bf16[1,2048,2048]{2,1,0:T(8,128)(2,1)} %get-tuple-element.16, bf16[2,512,2048]{2,1,0:T(8,128)(2,1)S(1)} %copy-done.2), kind=kOutput, calls=%fused_computation.5 | convolution fusion | flops 4297064448 | bytes 16777216 | tf_op jit(solution)/shard_map/dot_general | solution.py:548
  (27 shorter events, 4.3 us)
Async XLA Ops:
  0.0 19.2 %copy-start = (f32[3,3,2048]{2,1,0:T(4,128)S(1)}, f32[3,3,2048]{2,1,0:T(4,128)}, u32[]{:S(2)}) copy-start(f32[3,3,2048]{2,1,0:T(4,128)} %param.9) | copy-start | bytes 221188
  0.0 19.8 %copy-start.3 = (bf16[256,3,2048]{2,0,1:T(8,128)(2,1)S(1)}, bf16[256,3,2048]{2,0,1:T(8,128)(2,1)}, u32[]{:S(2)}) copy-start(bf16[256,3,2048]{2,0,1:T(8,128)(2,1)} %param.8) | copy-start | bytes 9437188
  1.6 28.2 %collective-permute-start = (bf16[2,4096]{1,0:T(2,128)(2,1)}, bf16[2,4096]{1,0:T(2,128)(2,1)}, u32[]{:S(2)}, u32[]{:S(2)}) collective-permute-start(bf16[2,4096]{1,0:T(2,128)(2,1)} %slice.9), channel_id=1, source_target_pairs={{0,2},{2,4},{4,6},{6,8},{8,10},{10,12},{12,14},{14,16},{16,18},{18... | collective-permute-start | bytes 49160 | tf_op jit(solution)/shard_map/ppermute | solution.py:20
  24.7 2.8 copy-start.4
  356.3 7.8 %copy-start.2 = (bf16[2,512,2048]{2,1,0:T(8,128)(2,1)S(1)}, bf16[2,512,2048]{2,1,0:T(8,128)(2,1)}, u32[]{:S(2)}) copy-start(bf16[2,512,2048]{2,1,0:T(8,128)(2,1)} %spread.1) | copy-start | bytes 12582916
  364.1 9.2 %copy-start.1 = (f32[3,3,2048]{2,1,0:T(4,128)S(1)}, f32[3,3,2048]{2,1,0:T(4,128)}, u32[]{:S(2)}) copy-start(f32[3,3,2048]{2,1,0:T(4,128)} %param.9) | copy-start | bytes 221188
